TPU v7x, 128 devices: a whole 4x4x4 slice. The times are simulated.
128 devices in a mesh: row: 8 (over z, y_lo), col: 16 (over y_hi, x, core).
Axes of the slice: x: 4, y: 4 (y_hi: 2, y_lo: 2; y = y_hi * 2 + y_lo), z: 4, core: 2. Of those that a mesh axis runs over, the one named last changes fastest.
Arguments:
- blocks: float32 [8, 16, 170, 128, 128], P('row', 'col'), may hold values from -1 to 1
- coords: int32 [8, 16, 2, 170], P('row', 'col'), may hold values from 0 to 31, as said below
- vectors: float32 [2, 32768, 128], P(None, ('row', 'col')), may hold values from -6 to 6
Outputs:
- basis: float32 [2, 32768, 128], P(None, ('row', 'col'))
Inputs may be any that keep to these rules, and one draw needn't show every extreme that they name: Within each tile the 170 listed positions are distinct, and the positions (0, 0) and (31, 15) are always listed; coords[r, c, 0, k] is below 32 and coords[r, c, 1, k] below 16.
All inputs are finite; a program needn't handle non-finite values.
Results may differ from a plain program's by a relative error of at most 0.0003.
Values sent between devices are 32-bit elements; how exact they have to be, the bound alone decides.
A program may use at most 192 MiB of HBM per device.

v0:
```python
import jax
import jax.numpy as jnp
from jax import lax
from jax.sharding import PartitionSpec as P

APPS = 2


exact_mode = lax.Precision.HIGHEST


def tile_products(values, places, col_side, row_side):
    blk_size = values.shape[1]
    listed = values.shape[0]
    row_blocks = row_side.shape[0] // blk_size
    col_blocks = col_side.shape[0] // blk_size
    row_of = places[0]
    col_of = places[1]
    col_pieces = col_side.reshape(col_blocks, blk_size, -1)[col_of]
    direct = jnp.einsum("kab,kbv->kav", values, col_pieces, precision=exact_mode)
    row_pieces = row_side.reshape(row_blocks, blk_size, -1)[row_of]
    flipped = jnp.einsum("kba,kbv->kav", values, row_pieces, precision=exact_mode)
    row_hot = (row_of[None, :] == jnp.arange(row_blocks, dtype=jnp.int32)[:, None]).astype(
        values.dtype
    )
    col_hot = (col_of[None, :] == jnp.arange(col_blocks, dtype=jnp.int32)[:, None]).astype(
        values.dtype
    )
    out_rows = jnp.dot(row_hot, direct.reshape(listed, -1), precision=exact_mode).reshape(
        row_side.shape[0], -1
    )
    out_cols = jnp.dot(col_hot, flipped.reshape(listed, -1), precision=exact_mode).reshape(
        col_side.shape[0], -1
    )
    return (out_rows, out_cols)


def normal_basis(applied, factor):
    return lax.linalg.triangular_solve(
        factor, applied, left_side=False, lower=True, transpose_a=True
    )


def local(blocks, coords, vectors):
    n_rowdev = lax.axis_size("row")
    n_coldev = lax.axis_size("col")
    group_rows = vectors.shape[1]
    total_rows = 2 * group_rows * n_rowdev * n_coldev
    values = blocks.reshape(blocks.shape[2], blocks.shape[3], blocks.shape[4])
    places = coords.reshape(2, coords.shape[3])
    start = (vectors[0], vectors[1])
    current = start
    for app_index in range(APPS):
        col_side = lax.all_gather(current[1], "row", axis=0, tiled=True)
        row_side = lax.all_gather(current[0], "col", axis=0, tiled=True)
        out_rows, out_cols = tile_products(values, places, col_side, row_side)
        new_upper = lax.psum_scatter(out_rows, "col", scatter_dimension=0, tiled=True)
        new_lower = lax.psum_scatter(out_cols, "row", scatter_dimension=0, tiled=True)
        applied = (new_upper, new_lower)
        factor_upper, factor_lower = applied
        partial_gram = jnp.einsum("nv,nw->vw", factor_upper, factor_upper, precision=exact_mode)
        partial_gram = partial_gram + jnp.einsum(
            "nv,nw->vw", factor_lower, factor_lower, precision=exact_mode
        )
        gram_sum = lax.psum(partial_gram, ("row", "col")) / total_rows
        factor = jnp.linalg.cholesky(gram_sum)
        current = (normal_basis(applied[0], factor), normal_basis(applied[1], factor))
    upper, lower = current
    return jnp.stack([upper, lower])


def solution(mesh):
    return jax.shard_map(
        local,
        mesh=mesh,
        in_specs=(
            P("row", "col", None, None, None),
            P("row", "col", None, None),
            P(None, ("row", "col"), None),
        ),
        out_specs=P(None, ("row", "col"), None),
        check_vma=False,
    )
```

profile of v0, /device:TPU:1, one launch (start us, length us, event | category | flops | bytes accessed | tf_op | source)
XLA Modules:
  0.0 845.5 jit_solution(6474394078749091209)
XLA Ops:
  10.6 37.6 %all-gather.11.cloned.1.call-done = f32[1,2048,128]{2,1,0:T(8,128)} async-done(((f32[1,256,128]{2,1,0:T(8,128)}), f32[1,2048,128]{2,1,0:T(8,128)}) %all-gather.11.cloned.1.call-update) | async-done | bytes 1048592 | tf_op jit(solution)/shard_map/all_gather | solution.py:54
  48.2 11.6 %gather_fusion = f32[170,128,128]{2,1,0:T(8,128)} fusion(f32[16,128,128]{2,1,0:T(8,128)} %bitcast.108, s32[1024]{0:T(1024)S(1)} %pad_clamp_fusion.1), kind=kCustom, calls=%fused_computation | custom fusion | bytes 22282920 | tf_op jit(solution)/shard_map/gather | solution.py:19
  59.8 23.3 %fusion.8 = f32[170,128,128]{1,2,0:T(8,128)} fusion(f32[170,128,128]{2,1,0:T(8,128)} %gather_fusion, f32[1,1,170,128,128]{4,3,2,1,0:T(8,128)} %param.6), kind=kOutput, calls=%fused_computation.12 | convolution fusion | flops 4278190080 | bytes 33423360 | tf_op jit(solution)/shard_map/kab,kbv->kav/dot_general | solution.py:20
  83.1 12.3 %copy.12 = f32[170,128,128]{2,1,0:T(8,128)} copy(f32[170,128,128]{1,2,0:T(8,128)} %fusion.8) | data formatting | bytes 22282240 | tf_op jit(solution)/shard_map/kab,kbv->kav/dot_general | solution.py:20
  95.3 10.5 %pad.6 = f32[176,128,128]{2,1,0:T(8,128)} pad(f32[170,128,128]{2,1,0:T(8,128)} %copy.12, f32[]{:T(128)} %constant.31.clone.2), padding=0_6x0_0x0_0 | pad | bytes 22675460
  105.8 18.3 %copy.38 = f32[22,8,128,128]{3,1,2,0:T(8,128)} copy(f32[22,8,128,128]{3,2,1,0:T(8,128)} %bitcast.115) | data formatting | bytes 23068672
  132.8 12.0 %gather_fusion.1 = f32[170,128,128]{2,1,0:T(8,128)} fusion(f32[32,128,128]{2,1,0:T(8,128)} %bitcast.110, s32[1024]{0:T(1024)S(1)} %pad_clamp_fusion), kind=kCustom, calls=%fused_computation.1 | custom fusion | bytes 22282920 | tf_op jit(solution)/shard_map/gather | solution.py:21
  144.8 23.4 %fusion.11 = f32[170,128,128]{1,2,0:T(8,128)} fusion(f32[170,128,128]{2,1,0:T(8,128)} %gather_fusion.1, f32[1,1,170,128,128]{4,3,2,1,0:T(8,128)} %param.6), kind=kOutput, calls=%fused_computation.13 | convolution fusion | flops 4278190080 | bytes 33423360 | tf_op jit(solution)/shard_map/kba,kbv->kav/dot_general | solution.py:22
  168.2 12.0 %copy.14 = f32[170,128,128]{2,1,0:T(8,128)} copy(f32[170,128,128]{1,2,0:T(8,128)} %fusion.11) | data formatting | bytes 22282240 | tf_op jit(solution)/shard_map/kba,kbv->kav/dot_general | solution.py:22
  180.3 10.4 %pad.7 = f32[176,128,128]{2,1,0:T(8,128)} pad(f32[170,128,128]{2,1,0:T(8,128)} %copy.14, f32[]{:T(128)} %constant.31.clone.2), padding=0_6x0_0x0_0 | pad | bytes 22675460
  190.7 18.4 %copy.39 = f32[22,8,128,128]{3,1,2,0:T(8,128)} copy(f32[22,8,128,128]{3,2,1,0:T(8,128)} %bitcast.117) | data formatting | bytes 23068672
  218.7 39.2 %reduce-scatter.7.cloned.1.call-done = f32[256,128]{1,0:T(8,128)} async-done(((f32[2048,128]{1,0:T(8,128)}), f32[256,128]{1,0:T(8,128)}) %reduce-scatter.7.cloned.1.call-update) | async-done | bytes 131088 | tf_op jit(solution)/shard_map/reduce_scatter | solution.py:58
  260.0 143.9 %all-reduce.3.cloned.1.call-done = f32[128,128]{0,1:T(8,128)} async-done(((f32[128,128]{0,1:T(8,128)}), f32[128,128]{0,1:T(8,128)}) %all-reduce.3.cloned.1.call-update) | async-done | bytes 65552 | tf_op jit(solution)/shard_map/psum | solution.py:65
  405.7 11.7 %cholesky.44 = f32[128,128]{1,0:T(8,128)S(1)} custom-call(f32[128,128]{1,0:T(8,128)S(1)} %fusion.27), custom_call_target="Cholesky" | custom-call | tf_op jit(solution)/shard_map/jit(cholesky)/cholesky | solution.py:66
  432.5 31.0 %all-gather.7.cloned.1.call-done = f32[2048,128]{0,1:T(8,128)} async-done(((f32[256,128]{0,1:T(8,128)}), f32[2048,128]{0,1:T(8,128)}) %all-gather.7.cloned.1.call-update) | async-done | bytes 1048592 | tf_op jit(solution)/shard_map/all_gather | solution.py:54
  470.3 23.5 %fusion.14 = f32[170,128,128]{1,2,0:T(8,128)} fusion(f32[170,128,128]{2,1,0:T(8,128)} %gather_fusion.2, f32[1,1,170,128,128]{4,3,2,1,0:T(8,128)} %param.6), kind=kOutput, calls=%fused_computation.14 | convolution fusion | flops 4278190080 | bytes 33423360 | tf_op jit(solution)/shard_map/kab,kbv->kav/dot_general | solution.py:20
  493.9 12.1 %copy.20 = f32[170,128,128]{2,1,0:T(8,128)} copy(f32[170,128,128]{1,2,0:T(8,128)} %fusion.14) | data formatting | bytes 22282240 | tf_op jit(solution)/shard_map/kab,kbv->kav/dot_general | solution.py:20
  516.3 18.4 %copy.40 = f32[22,8,128,128]{3,1,2,0:T(8,128)} copy(f32[22,8,128,128]{3,2,1,0:T(8,128)} %bitcast.118) | data formatting | bytes 23068672
  550.8 23.4 %fusion.17 = f32[170,128,128]{1,2,0:T(8,128)} fusion(f32[170,128,128]{2,1,0:T(8,128)} %gather_fusion.3, f32[1,1,170,128,128]{4,3,2,1,0:T(8,128)} %param.6), kind=kOutput, calls=%fused_computation.15 | convolution fusion | flops 4278190080 | bytes 33423360 | tf_op jit(solution)/shard_map/kba,kbv->kav/dot_general | solution.py:22
  574.2 12.0 %copy.23 = f32[170,128,128]{2,1,0:T(8,128)} copy(f32[170,128,128]{1,2,0:T(8,128)} %fusion.17) | data formatting | bytes 22282240 | tf_op jit(solution)/shard_map/kba,kbv->kav/dot_general | solution.py:22
  596.6 18.3 %copy.41 = f32[22,8,128,128]{3,1,2,0:T(8,128)} copy(f32[22,8,128,128]{3,2,1,0:T(8,128)} %bitcast.113) | data formatting | bytes 23068672
  624.3 39.3 %reduce-scatter.11.cloned.1.call-done = f32[256,128]{1,0:T(8,128)} async-done(((f32[2048,128]{1,0:T(8,128)}), f32[256,128]{1,0:T(8,128)}) %reduce-scatter.11.cloned.1.call-update) | async-done | bytes 131088 | tf_op jit(solution)/shard_map/reduce_scatter | solution.py:58
  665.6 144.9 %all-reduce.5.cloned.1.call-done = f32[128,128]{0,1:T(8,128)} async-done(((f32[128,128]{0,1:T(8,128)}), f32[128,128]{0,1:T(8,128)}) %all-reduce.5.cloned.1.call-update) | async-done | bytes 65552 | tf_op jit(solution)/shard_map/psum | solution.py:65
  812.3 11.7 %cholesky.55 = f32[128,128]{1,0:T(8,128)S(1)} custom-call(f32[128,128]{1,0:T(8,128)S(1)} %fusion.24), custom_call_target="Cholesky" | custom-call | tf_op jit(solution)/shard_map/jit(cholesky)/cholesky | solution.py:66
  (67 shorter events, 112.4 us)
Async XLA Ops:
  6.5 41.7 %all-gather.11.cloned.1.call-start = ((), (), s32[]{:S(2)}) async-start(), calls=%async_computation.12 | async-start | bytes 1179648 | tf_op jit(solution)/shard_map/all_gather | solution.py:54
  8.2 124.6 %all-gather.13.cloned.1.call-start = ((), (), s32[]{:S(2)}) async-start(), calls=%async_computation.13 | async-start | bytes 2228224 | tf_op jit(solution)/shard_map/all_gather | solution.py:55
  9.0 208.3 %reduce-scatter.5.cloned.1.call-start = ((), (), s32[]{:S(2)}) async-start(), calls=%async_computation.4 | async-start | bytes 2228224 | tf_op jit(solution)/shard_map/reduce_scatter | solution.py:57
  132.7 125.2 %reduce-scatter.7.cloned.1.call-start = ((), (), s32[]{:S(2)}) async-start(), calls=%async_computation.5 | async-start | bytes 1179648 | tf_op jit(solution)/shard_map/reduce_scatter | solution.py:58
  217.2 186.7 %all-reduce.3.cloned.1.call-start = ((), (), s32[]{:S(2)}) async-start(), calls=%async_computation.6 | async-start | bytes 131072 | tf_op jit(solution)/shard_map/psum | solution.py:65
  259.9 203.5 %all-gather.7.cloned.1.call-start = ((), (), s32[]{:S(2)}) async-start(), calls=%async_computation.7 | async-start | bytes 1179648 | tf_op jit(solution)/shard_map/all_gather | solution.py:54
  430.5 113.1 %all-gather.9.cloned.1.call-start = ((), (), s32[]{:S(2)}) async-start(), calls=%async_computation.9 | async-start | bytes 2228224 | tf_op jit(solution)/shard_map/all_gather | solution.py:55
  432.4 190.5 %reduce-scatter.9.cloned.1.call-start = ((), (), s32[]{:S(2)}) async-start(), calls=%async_computation.8 | async-start | bytes 2228224 | tf_op jit(solution)/shard_map/reduce_scatter | solution.py:57
  543.5 120.1 %reduce-scatter.11.cloned.1.call-start = ((), (), s32[]{:S(2)}) async-start(), calls=%async_computation.10 | async-start | bytes 1179648 | tf_op jit(solution)/shard_map/reduce_scatter | solution.py:58
  622.9 187.6 %all-reduce.5.cloned.1.call-start = ((), (), s32[]{:S(2)}) async-start(), calls=%async_computation.11 | async-start | bytes 131072 | tf_op jit(solution)/shard_map/psum | solution.py:65
Sparse Core Ops, SparseCore 0:
  9.0 39.1 all-gather.10
  50.6 52.7 all-gather.12
  132.9 72.9 reduce-scatter.4
  217.4 40.5 reduce-scatter.6
  262.5 141.3 all-reduce.2
  430.6 32.8 all-gather.6
  466.0 53.9 all-gather.8
  543.6 73.1 reduce-scatter.8
  623.0 40.5 reduce-scatter.10
  668.9 141.5 all-reduce.4
where the time goes:
time: 855 us; the launch traced here: 846 us
  waiting for transfers between devices  437 us (51%)
  local copies, waits for them, and re-layouts  210 us (25%)
  matrix products  135 us (16%)
  other arithmetic  49.9 us (6%)
  between operations  14 us (2%)
    psum x2, waiting for transfers between devices, local(): gram_sum = lax.psum(partial_gram, ('row', 'col')) / total_rows  289 us
    unnamed x8, local copies, waits for them, and re-layouts  115 us
    reduce_scatter x2, waiting for transfers between devices, local(): lax.psum_scatter(out_cols, 'row', scatter_dimension=0, tiled=True)  78.5 us
    all_gather x2, waiting for transfers between devices, local(): col_side = lax.all_gather(current[1], 'row', axis=0, tiled=True)  68.6 us
    dot_general x2, matrix products, tile_products(): jnp.einsum('kab,kbv->kav', values, col_pieces, precision=exact_mode)  46.9 us
    dot_general x2, matrix products, tile_products(): jnp.einsum('kba,kbv->kav', values, row_pieces, precision=exact_mode)  46.8 us
    another operation x6, other arithmetic, local(): factor = jnp.linalg.cholesky(gram_sum)  24.8 us
    dot_general x2, local copies, waits for them, and re-layouts, tile_products(): jnp.einsum('kab,kbv->kav', values, col_pieces, precision=exact_mode)  24.3 us
  transfers between devices with their start and end apart: 10, of which 6 were waited for; matrix products, arithmetic and copies ran while one was open for 40% of the time, Pallas kernels for 0%

commit v1 on v0

v1 whole, which is shorter than its diff:
```python
import functools

import jax
import jax.numpy as jnp
from jax import lax
from jax.experimental import pallas as pl
from jax.experimental.pallas import tpu as pltpu
from jax.sharding import PartitionSpec as P

MESH = pl.DeviceIdType.MESH
HIGH = lax.Precision.HIGHEST
F32 = jnp.float32
BF16 = jnp.bfloat16

GROUP = 256
NV = 128
BLK = 128
NROW = 8
NCOL = 16
CHUNK = 10
LIFT = 2.0**20


class Where:
    def __init__(self):
        self.r = lax.axis_index("row")
        self.c = lax.axis_index("col")
        self.z = self.r // 2
        self.yl = self.r % 2
        self.yh = self.c // 8
        self.x = (self.c // 2) % 4
        self.core = self.c % 2

    def zr(self, dz, other=False):
        yl = 1 - self.yl if other else self.yl
        return ((self.z + dz) % 4) * 2 + yl

    def xc(self, dx, other_y=False, other_core=False):
        yh = 1 - self.yh if other_y else self.yh
        core = 1 - self.core if other_core else self.core
        return (yh * 4 + (self.x + dx) % 4) * 2 + core

    def neighbours(self):
        out = [(self.zr(dz), self.c) for dz in (1, 2, 3)]
        out.append((self.zr(0, True), self.c))
        out += [(self.r, self.xc(dx)) for dx in (1, 2, 3)]
        out.append((self.r, self.xc(0, True)))
        out.append((self.r, self.xc(0, False, True)))
        return out

    def all_group(self):
        out = [((self.r + d) % NROW, self.c) for d in range(1, NROW)]
        out += [(self.r, (self.c + d) % NCOL) for d in range(1, NCOL)]
        return out


def entry_barrier(partners):
    barrier = pltpu.get_barrier_semaphore()
    for p in partners:
        pl.semaphore_signal(barrier, inc=1, device_id=p, device_id_type=MESH)
    pl.semaphore_wait(barrier, len(partners))


def rcopy(src, dst, send, recv, dev):
    return pltpu.make_async_remote_copy(
        src_ref=src,
        dst_ref=dst,
        send_sem=send,
        recv_sem=recv,
        device_id=dev,
        device_id_type=MESH,
    )


class Gather:
    def __init__(self, w, up, lo, rowbuf, colbuf, su, ru, sl, rl):
        self.w, self.up, self.lo = w, up, lo
        self.rowbuf, self.colbuf = rowbuf, colbuf
        self.su, self.ru, self.sl, self.rl = su, ru, sl, rl
        self.sent = []
        self.nu = 0
        self.nl = 0

    def send_u(self, src, piece, dev):
        cp = rcopy(src, self.rowbuf.at[piece], self.su.at[self.nu], self.ru.at[piece], dev)
        self.nu += 1
        cp.start()
        self.sent.append(cp)

    def send_l(self, src, piece, dev):
        cp = rcopy(src, self.colbuf.at[piece], self.sl.at[self.nl], self.rl.at[piece], dev)
        self.nl += 1
        cp.start()
        self.sent.append(cp)

    def wait_u(self, piece):
        ref = self.rowbuf.at[piece]
        rcopy(ref, ref, self.su.at[0], self.ru.at[piece], (self.w.r, self.w.xc(0, True))).wait_recv()

    def wait_l(self, piece):
        ref = self.colbuf.at[piece]
        rcopy(ref, ref, self.sl.at[0], self.rl.at[piece], (self.w.zr(0, True), self.w.c)).wait_recv()

    def start(self):
        w = self.w
        self.send_u(self.up, w.c, (w.r, w.xc(0, True)))
        self.send_l(self.lo, w.r, (w.zr(0, True), w.c))
        for d in (2, 1, 3):
            self.send_u(self.up, w.c, (w.r, w.xc(d)))
            self.send_l(self.lo, w.r, (w.zr(d), w.c))
        self.send_u(self.up, w.c, (w.r, w.xc(0, False, True)))
        self.rowbuf[w.c] = self.up[...]
        self.colbuf[w.r] = self.lo[...]

    def forward_y(self):
        w = self.w
        pu = w.xc(0, True)
        ql = w.zr(0, True)
        self.wait_l(ql)
        for d in (2, 1, 3):
            self.send_l(self.colbuf.at[ql], ql, (w.zr(d), w.c))
        self.wait_u(pu)
        for d in (2, 1, 3):
            self.send_u(self.rowbuf.at[pu], pu, (w.r, w.xc(d)))
        self.send_u(self.rowbuf.at[pu], pu, (w.r, w.xc(0, False, True)))

    def forward_x(self, other_y):
        w = self.w
        for d in (1, 3, 2):
            p = w.xc(d, other_y)
            self.wait_u(p)
            self.send_u(self.rowbuf.at[p], p, (w.r, w.xc(0, False, True)))

    def finish(self):
        w = self.w
        for other in (False, True):
            for d in (1, 2, 3):
                self.wait_l(w.zr(d, other))
        for other in (False, True):
            for d in (0, 1, 2, 3):
                self.wait_u(w.xc(d, other, True))
        for cp in self.sent:
            cp.wait_send()


def gather_kernel(vec, rowbuf, colbuf, su, ru, sl, rl):
    w = Where()
    entry_barrier(w.neighbours())
    g = Gather(w, vec.at[0], vec.at[1], rowbuf, colbuf, su, ru, sl, rl)
    g.start()
    g.forward_y()
    g.forward_x(False)
    g.forward_x(True)
    g.finish()


GATHER_SEMS = [
    pltpu.SemaphoreType.DMA((15,)),
    pltpu.SemaphoreType.DMA((16,)),
    pltpu.SemaphoreType.DMA((7,)),
    pltpu.SemaphoreType.DMA((8,)),
]


def reduce_scatter(w, rows, cols, acc, sib, xbuf, yhbuf, zbuf, ylbuf, mid, s_s, r_s, s_x, r_x, s_z, r_z, s_y, r_y, between=None):
    sent = []
    sibling = (w.r, w.xc(0, False, True))
    order = [(d, o) for d in (2, 1, 3, 0) for o in (True, False)]
    for i, (d, o) in enumerate(order):
        cp = rcopy(rows.at[w.xc(d, o, True)], sib.at[i], s_s.at[i], r_s.at[i], sibling)
        cp.start()
        sent.append(cp)
    for i, d in enumerate((2, 1, 3)):
        for j, o in enumerate((True, False)):
            cp = rcopy(cols.at[w.zr(d, o)], zbuf.at[i, j], s_z.at[i, j], r_z.at[i, j], (w.zr(d), w.c))
            cp.start()
            sent.append(cp)
    for i, (d, o) in enumerate(order):
        sent[i].wait_recv()
        acc[i] = rows[w.xc(d, o)] + sib[i]
        if d:
            k, j = i // 2, i % 2
            cp = rcopy(acc.at[i], xbuf.at[k, j], s_x.at[k, j], r_x.at[k, j], (w.r, w.xc(d)))
            cp.start()
            sent.append(cp)
    zc = [c for c in sent[8:14]]
    xc = [c for c in sent[14:20]]
    if between is not None:
        between()
    for i in range(3):
        zc[2 * i].wait_recv()
    mid[0] = cols[w.zr(0, True)] + zbuf[0, 0] + zbuf[1, 0] + zbuf[2, 0]
    cl = rcopy(mid.at[0], ylbuf, s_y.at[0], r_y.at[0], (w.zr(0, True), w.c))
    cl.start()
    for i in range(3):
        xc[2 * i].wait_recv()
    mid[1] = acc[6] + xbuf[0, 0] + xbuf[1, 0] + xbuf[2, 0]
    cu = rcopy(mid.at[1], yhbuf, s_y.at[1], r_y.at[1], (w.r, w.xc(0, True)))
    cu.start()
    for i in range(3):
        zc[2 * i + 1].wait_recv()
    lower = cols[w.zr(0)] + zbuf[0, 1] + zbuf[1, 1] + zbuf[2, 1]
    mid[2] = lower
    for i in range(3):
        xc[2 * i + 1].wait_recv()
    mid[3] = acc[7] + xbuf[0, 1] + xbuf[1, 1] + xbuf[2, 1]
    cl.wait_recv()
    lower = mid[2] + ylbuf[...]
    cu.wait_recv()
    upper = mid[3] + yhbuf[...]
    for cp in sent:
        cp.wait_send()
    cl.wait_send()
    cu.wait_send()
    return upper, lower


RS_SCRATCH = [
    pltpu.VMEM((8, GROUP, NV), F32),
    pltpu.VMEM((8, GROUP, NV), F32),
    pltpu.VMEM((3, 2, GROUP, NV), F32),
    pltpu.VMEM((GROUP, NV), F32),
    pltpu.VMEM((3, 2, GROUP, NV), F32),
    pltpu.VMEM((GROUP, NV), F32),
    pltpu.VMEM((4, GROUP, NV), F32),
    pltpu.SemaphoreType.DMA((8,)),
    pltpu.SemaphoreType.DMA((8,)),
    pltpu.SemaphoreType.DMA((3, 2)),
    pltpu.SemaphoreType.DMA((3, 2)),
    pltpu.SemaphoreType.DMA((3, 2)),
    pltpu.SemaphoreType.DMA((3, 2)),
    pltpu.SemaphoreType.DMA((2,)),
    pltpu.SemaphoreType.DMA((2,)),
]


class GramSum:
    def __init__(self, w, part, g1, s1, g2, s2, full, ss, rr):
        self.w, self.part, self.g1, self.s1, self.g2, self.s2, self.full = w, part, g1, s1, g2, s2, full
        self.ss, self.rr = ss, rr
        self.sent = []

    def exchange(self, lo, count, src_of, dst, me, dev_of):
        cps = []
        for d in range(1, count):
            cp = rcopy(src_of(d), dst.at[me], self.ss.at[lo + d], self.rr.at[lo + d], dev_of(d))
            cp.start()
            cps.append(cp)
        self.sent += cps
        return cps

    def phase1(self):
        w = self.w

        def src(d):
            return self.part.at[(w.c + d) % NCOL]

        self.cps = self.exchange(0, NCOL, src, self.g1, w.c, lambda d: (w.r, (w.c + d) % NCOL))
        self.g1[w.c] = self.part[w.c]

    def phase2(self):
        w = self.w
        for cp in self.cps:
            cp.wait_recv()
        total = self.g1[0]
        for i in range(1, NCOL):
            total = total + self.g1[i]
        self.s1[...] = total
        self.cps = self.exchange(NCOL, NROW, lambda d: self.s1, self.g2, w.r, lambda d: ((w.r + d) % NROW, w.c))
        self.g2[w.r] = total

    def phase3(self):
        w = self.w
        for cp in self.cps:
            cp.wait_recv()
        total = self.g2[0]
        for i in range(1, NROW):
            total = total + self.g2[i]
        total = total * (1.0 / (2 * GROUP * NROW * NCOL))
        self.s2[...] = total
        self.cps = self.exchange(
            NCOL + NROW, NCOL, lambda d: self.s2, self.full, w.c, lambda d: (w.r, (w.c + d) % NCOL)
        )
        self.full[w.c] = total

    def finish(self):
        for cp in self.cps:
            cp.wait_recv()
        for cp in self.sent:
            cp.wait_send()


GRAM_SCRATCH = [
    pltpu.VMEM((NCOL, 8, NV), F32),
    pltpu.VMEM((NCOL, 8, NV), F32),
    pltpu.VMEM((8, NV), F32),
    pltpu.VMEM((NROW, 8, NV), F32),
    pltpu.VMEM((8, NV), F32),
    pltpu.SemaphoreType.DMA((2 * NCOL + NROW,)),
    pltpu.SemaphoreType.DMA((2 * NCOL + NROW,)),
]


def self_product(v):
    return lax.dot_general(v, v, (((0,), (0,)), ((), ())), precision=HIGH, preferred_element_type=F32)


def middle_kernel(rows, cols, rowbuf, colbuf, gram, acc, sib, xbuf, yhbuf, zbuf, ylbuf, mid, s_s, r_s, s_x, r_x, s_z, r_z, s_y, r_y, both, su, ru, sl, rl, part, g1, s1, g2, s2, ss, rr):
    w = Where()
    entry_barrier(w.all_group())
    upper, lower = reduce_scatter(w, rows, cols, acc, sib, xbuf, yhbuf, zbuf, ylbuf, mid, s_s, r_s, s_x, r_x, s_z, r_z, s_y, r_y)
    both[0] = upper * LIFT
    both[1] = lower * LIFT
    g = Gather(w, both.at[0], both.at[1], rowbuf, colbuf, su, ru, sl, rl)
    g.start()
    part[...] = (self_product(both[0]) + self_product(both[1])).reshape(NCOL, 8, NV)
    s = GramSum(w, part, g1, s1, g2, s2, gram, ss, rr)
    s.phase1()
    g.forward_y()
    s.phase2()
    g.forward_x(False)
    s.phase3()
    g.forward_x(True)
    g.finish()
    s.finish()


def times_inverse(v, linv):
    return lax.dot_general(v, linv, (((1,), (1,)), ((), ())), precision=HIGH, preferred_element_type=F32)


def last_kernel(rows, cols, linv, out, gram, acc, sib, xbuf, yhbuf, zbuf, ylbuf, mid, s_s, r_s, s_x, r_x, s_z, r_z, s_y, r_y, part, g1, s1, g2, s2, ss, rr):
    w = Where()
    entry_barrier(w.all_group())
    upper, lower = reduce_scatter(w, rows, cols, acc, sib, xbuf, yhbuf, zbuf, ylbuf, mid, s_s, r_s, s_x, r_x, s_z, r_z, s_y, r_y)
    out[0] = times_inverse(upper, linv[...])
    out[1] = times_inverse(lower, linv[...])
    part[...] = (self_product(out[0]) + self_product(out[1])).reshape(NCOL, 8, NV)
    s = GramSum(w, part, g1, s1, g2, s2, gram, ss, rr)
    s.phase1()
    s.phase2()
    s.phase3()
    s.finish()


def inverse_factor(gram):
    tiles = [gram[t * 8 : t * 8 + 8, :] for t in range(16)]
    lane = lax.broadcasted_iota(jnp.int32, (8, NV), 1)
    sub = lax.broadcasted_iota(jnp.int32, (8, NV), 0)
    for j in range(NV):
        t0, i0 = j // 8, j % 8
        here = lane == j
        row = tiles[t0][i0 : i0 + 1, :]
        inv = 1.0 / row[:, j : j + 1]
        step = jnp.where(here[0:1], 1.0, row) * inv
        for t in range(t0, 16):
            tile = tiles[t]
            col = jnp.broadcast_to(tile[:, j : j + 1], (8, NV))
            new = jnp.where(here, 0.0, tile) - col * step
            tiles[t] = jnp.where(sub > i0, new, tile) if t == t0 else new
    out = []
    for t in range(16):
        tile = tiles[t]
        diag = jnp.sum(jnp.where(lane == sub + 8 * t, tile, 0.0), axis=1, keepdims=True)
        unit = jnp.where(lane < sub + 8 * t, tile, jnp.where(lane == sub + 8 * t, 1.0, 0.0))
        out.append(unit * (1.0 / jnp.sqrt(diag)))
    return jnp.concatenate(out, axis=0)


def factor_kernel(gram, linv):
    linv[...] = inverse_factor(gram[...].reshape(NV, NV))


def finish_kernel(gram, y, out):
    linv = inverse_factor(gram[...].reshape(NV, NV))
    out[0] = times_inverse(y[0], linv)
    out[1] = times_inverse(y[1], linv)


def split(v):
    hi = v.astype(BF16)
    lo = (v - hi.astype(F32)).astype(BF16)
    return hi, lo


def product_kernel(places, blocks, row_side, col_side, rows, cols, wcol, xrow, flipped):
    step = pl.program_id(0)

    @pl.when(step == 0)
    def _():
        @pl.loop(0, 16)
        def _(i):
            hi, lo = split(col_side[i])
            wcol[i] = jnp.concatenate([jnp.concatenate([hi, lo], axis=1)] * 2, axis=0)
            flipped[i] = jnp.zeros((NV, BLK), F32)

        @pl.loop(0, 32)
        def _(i):
            hi, lo = split(row_side[i].T)
            xrow[i] = jnp.concatenate([hi, lo], axis=1)
            rows[i] = jnp.zeros((BLK, NV), F32)

    for b in range(CHUNK):
        k = step * CHUNK + b
        r = places[0, k]
        c = places[1, k]
        hi, lo = split(blocks[b])
        flat = jnp.concatenate([hi, lo], axis=1)
        d = jnp.dot(flat, wcol[c], preferred_element_type=F32)
        rows[r] += d[:, :NV] + d[:, NV:]
        e = jnp.dot(xrow[r], jnp.concatenate([flat, flat], axis=0), preferred_element_type=F32)
        flipped[c] += e[:, :BLK] + e[:, BLK:]

    @pl.when(step == pl.num_programs(0) - 1)
    def _():
        @pl.loop(0, 16)
        def _(i):
            cols[i] = flipped[i].T


def products(values, places, rowbuf, colbuf):
    listed = values.shape[0]
    whole = lambda n: pl.BlockSpec((n, BLK, NV), lambda i, p: (0, 0, 0), pipeline_mode=pl.Buffered(1))
    rows, cols = pl.pallas_call(
        product_kernel,
        out_shape=(
            jax.ShapeDtypeStruct((32, BLK, NV), F32),
            jax.ShapeDtypeStruct((16, BLK, NV), F32),
        ),
        grid_spec=pltpu.PrefetchScalarGridSpec(
            num_scalar_prefetch=1,
            grid=(listed // CHUNK,),
            in_specs=[
                pl.BlockSpec((CHUNK, BLK, BLK), lambda i, p: (i, 0, 0)),
                whole(32),
                whole(16),
            ],
            out_specs=(whole(32), whole(16)),
            scratch_shapes=[
                pltpu.VMEM((16, 2 * BLK, 2 * NV), BF16),
                pltpu.VMEM((32, NV, 2 * BLK), BF16),
                pltpu.VMEM((16, NV, BLK), F32),
            ],
        ),
        compiler_params=pltpu.CompilerParams(vmem_limit_bytes=40 << 20),
        name="tile_products",
    )(places, values, rowbuf.reshape(32, BLK, NV), colbuf.reshape(16, BLK, NV))
    return rows.reshape(NCOL, GROUP, NV), cols.reshape(NROW, GROUP, NV)


VM = pl.BlockSpec(memory_space=pltpu.VMEM)


def remote_call(kernel, name, cid, ins, outs, scratch):
    return pl.pallas_call(
        kernel,
        out_shape=tuple(jax.ShapeDtypeStruct(s, F32) for s in outs),
        in_specs=[VM] * ins,
        out_specs=tuple([VM] * len(outs)),
        scratch_shapes=scratch,
        compiler_params=pltpu.CompilerParams(
            collective_id=cid, has_side_effects=True, vmem_limit_bytes=40 << 20
        ),
        name=name,
    )


def local(blocks, coords, vectors):
    values = blocks.reshape(blocks.shape[2], BLK, BLK)
    places = coords.reshape(2, coords.shape[3])
    row_shape = (NCOL, GROUP, NV)
    col_shape = (NROW, GROUP, NV)
    gram_shape = (NCOL, 8, NV)
    rowbuf, colbuf = remote_call(gather_kernel, "gather", 0, 1, [row_shape, col_shape], GATHER_SEMS)(vectors)
    rows, cols = products(values, places, rowbuf, colbuf)
    rowbuf, colbuf, gram = remote_call(
        middle_kernel,
        "middle",
        1,
        2,
        [row_shape, col_shape, gram_shape],
        RS_SCRATCH + [pltpu.VMEM((2, GROUP, NV), F32)] + GATHER_SEMS + GRAM_SCRATCH,
    )(rows, cols)
    linv = pl.pallas_call(
        factor_kernel,
        out_shape=jax.ShapeDtypeStruct((NV, NV), F32),
        name="factor",
    )(gram)
    rows, cols = products(values, places, rowbuf, colbuf)
    y, gram = remote_call(
        last_kernel,
        "last",
        2,
        3,
        [(2, GROUP, NV), gram_shape],
        RS_SCRATCH + GRAM_SCRATCH,
    )(rows, cols, linv)
    return pl.pallas_call(
        finish_kernel,
        out_shape=jax.ShapeDtypeStruct((2, GROUP, NV), F32),
        name="finish",
    )(gram, y)


def solution(mesh):
    return jax.shard_map(
        local,
        mesh=mesh,
        in_specs=(
            P("row", "col", None, None, None),
            P("row", "col", None, None),
            P(None, ("row", "col"), None),
        ),
        out_specs=P(None, ("row", "col"), None),
        check_vma=False,
    )
```

time: 855 us -> 175 us (0.20); the launches traced: 846 us -> 174 us
  waiting for transfers between devices: 437 us -> 0 us
  local copies, waits for them, and re-layouts: 210 us -> 3.79 us
  Pallas kernels: 0 us -> 170 us
  matrix products: 135 us -> 0 us
  other arithmetic: 49.9 us -> 0 us
  between operations: 14 us -> 0.09 us
    psum x2 -> x0, waiting for transfers between devices: 289 us -> none  [local(): gram_sum = lax.psum(partial_gram, ('row', 'col')) / total_rows]
    pallas_call x0 -> x7, Pallas kernels: none -> 170 us  [the longest x1 43.8 us: local(): remote_call(middle_kernel, 'middle', 1, 2, [row_shape, col_shape, gram_sh...]
    dot_general x12 -> x0, matrix products: 128 us -> none  [the longest x2 46.9 us: tile_products(): jnp.einsum('kab,kbv->kav', values, col_pieces, precision=exact_mode)]
    unnamed x8 -> x14, local copies, waits for them, and re-layouts: 115 us -> 3.79 us
    reduce_scatter x4 -> x0, waiting for transfers between devices: 78.6 us -> none  [the longest x2 78.5 us: local(): lax.psum_scatter(out_cols, 'row', scatter_dimension=0, tiled=True)]
    all_gather x4 -> x0, waiting for transfers between devices: 68.6 us -> none  [the longest x2 68.6 us: local(): col_side = lax.all_gather(current[1], 'row', axis=0, tiled=True)]
    dot_general x4 -> x0, local copies, waits for them, and re-layouts: 48.3 us -> none  [the longest x2 24.3 us: tile_products(): jnp.einsum('kab,kbv->kav', values, col_pieces, precision=exact_mode)]
    another operation x11 -> x0, other arithmetic: 45.7 us -> none  [the longest x6 24.8 us: local(): factor = jnp.linalg.cholesky(gram_sum)]
  transfers between devices with their start and end apart: 10 -> 0, of which waited for: 6 -> 0; matrix products, arithmetic and copies ran while one was open for 40% -> 0% of each run, Pallas kernels for 0% -> 0%
where the time goes in v1:
time: 175 us; the launch traced here: 174 us
  Pallas kernels  170 us (97%)
  local copies, waits for them, and re-layouts  3.79 us (2%)
    pallas_call x1, Pallas kernels, local(): remote_call(middle_kernel, 'middle', 1, 2, [row_shape, col_shape, gram_sh...  43.8 us
    pallas_call x2, Pallas kernels, products(): pl.pallas_call(product_kernel, out_shape=(jax.ShapeDtypeStruct((32, BLK,...  41.3 us
    pallas_call x1, Pallas kernels, local(): remote_call(last_kernel, 'last', 2, 3, [(2, GROUP, NV), gram_shape], RS_S...  37.2 us
    pallas_call x1, Pallas kernels, local(): remote_call(gather_kernel, 'gather', 0, 1, [row_shape, col_shape], GATHER...  22.8 us
    pallas_call x1, Pallas kernels, local(): pl.pallas_call(finish_kernel, out_shape=jax.ShapeDtypeStruct((2, GROUP, N...  12.9 us
    pallas_call x1, Pallas kernels, local(): pl.pallas_call(factor_kernel, out_shape=jax.ShapeDtypeStruct((NV, NV), F3...  12.3 us
    unnamed x14, local copies, waits for them, and re-layouts  3.79 us

profile of v1, /device:TPU:1, one launch (start us, length us, event | category | flops | bytes accessed | tf_op | source)
XLA Modules:
  0.0 174.1 jit_solution(1400421327415805818)
XLA Ops:
  0.0 0.0 copy-start.1
  0.0 0.9 copy-done.1
  1.0 22.8 %gather.1 = (f32[16,256,128]{2,1,0:T(8,128)S(1)}, f32[8,256,128]{2,1,0:T(8,128)S(1)}) custom-call(f32[2,256,128]{2,1,0:T(8,128)S(1)} %copy-done.1), custom_call_target="tpu_custom_call" | custom-call | tf_op jit(solution)/shard_map/gather/pallas_call | solution.py:474
  23.8 0.0 copy-start.5
  23.8 0.7 copy-done.5
  24.4 20.7 %tile_products.2 = (f32[32,128,128]{2,1,0:T(8,128)S(1)}, f32[16,128,128]{2,1,0:T(8,128)S(1)}) custom-call(s32[2,170]{1,0:T(2,128)S(1)} %bitcast.18, f32[170,128,128]{2,1,0:T(8,128)} %bitcast.20, f32[32,128,128]{2,1,0:T(8,128)S(1)} %bitcast.13, f32[16,128,128]{2,1,0:T(8,128)S(1)} %bitcast.17), custom_call_target="tpu_custom_call" | custom-call | tf_op jit(solution)/shard_map/tile_products/pallas_call | solution.py:424
  45.1 0.0 copy-start.6
  45.1 43.8 %middle.1 = (f32[16,256,128]{2,1,0:T(8,128)S(1)}, f32[8,256,128]{2,1,0:T(8,128)S(1)}, f32[16,8,128]{2,1,0:T(8,128)S(1)}) custom-call(f32[16,256,128]{2,1,0:T(8,128)S(1)} %bitcast.10, f32[8,256,128]{2,1,0:T(8,128)S(1)} %bitcast.15), custom_call_target="tpu_custom_call" | custom-call | tf_op jit(solution)/shard_map/middle/pallas_call | solution.py:476
  88.9 0.0 copy-start.4
  88.9 0.0 copy-done.6
  88.9 20.7 %tile_products.3 = (f32[32,128,128]{2,1,0:T(8,128)S(1)}, f32[16,128,128]{2,1,0:T(8,128)S(1)}) custom-call(s32[2,170]{1,0:T(2,128)S(1)} %bitcast.19, f32[170,128,128]{2,1,0:T(8,128)} %bitcast.21, f32[32,128,128]{2,1,0:T(8,128)S(1)} %bitcast.12, f32[16,128,128]{2,1,0:T(8,128)S(1)} %bitcast.16), custom_call_target="tpu_custom_call" | custom-call | tf_op jit(solution)/shard_map/tile_products/pallas_call | solution.py:424
  109.6 0.0 copy-done.4
  109.6 12.3 %factor.1.linv = f32[128,128]{1,0:T(8,128)} custom-call(f32[16,8,128]{2,1,0:T(8,128)} %copy-done.4), custom_call_target="tpu_custom_call" | custom-call | tf_op jit(solution)/shard_map/factor/pallas_call | solution.py:484
  121.9 0.0 copy-start
  121.9 0.8 copy-done
  122.7 37.2 %last.1 = (f32[2,256,128]{2,1,0:T(8,128)S(1)}, f32[16,8,128]{2,1,0:T(8,128)S(1)}) custom-call(f32[16,256,128]{2,1,0:T(8,128)S(1)} %bitcast.11, f32[8,256,128]{2,1,0:T(8,128)S(1)} %bitcast.14, f32[128,128]{1,0:T(8,128)S(1)} %copy-done), custom_call_target="tpu_custom_call" | custom-call | tf_op jit(solution)/shard_map/last/pallas_call | solution.py:490
  159.9 0.0 copy-start.2
  159.9 0.7 copy-done.2
  160.6 0.0 copy-start.3
  160.6 0.6 copy-done.3
  161.3 12.9 %finish.1 = f32[2,256,128]{2,1,0:T(8,128)} custom-call(f32[16,8,128]{2,1,0:T(8,128)} %copy-done.3, f32[2,256,128]{2,1,0:T(8,128)} %copy-done.2), custom_call_target="tpu_custom_call" | custom-call | tf_op jit(solution)/shard_map/finish/pallas_call | solution.py:498
Async XLA Ops:
  0.0 0.9 copy-start.1
  23.8 0.7 copy-start.5
  45.1 43.8 %copy-start.6 = (s32[1,1,2,170]{3,2,1,0:T(2,128)S(1)}, s32[1,1,2,170]{3,2,1,0:T(2,128)}, u32[]{:S(2)}) copy-start(s32[1,1,2,170]{3,2,1,0:T(2,128)} %param.4) | copy-start | bytes 4084
  88.9 20.7 %copy-start.4 = (f32[16,8,128]{2,1,0:T(8,128)}, f32[16,8,128]{2,1,0:T(8,128)S(1)}, u32[]{:S(2)}) copy-start(f32[16,8,128]{2,1,0:T(8,128)S(1)} %get-tuple-element.24.gram) | copy-start | bytes 196612
  121.9 0.8 copy-start
  159.9 0.7 copy-start.2
  160.6 0.6 copy-start.3

commit v2 on v1

--- a/solution.py
+++ b/solution.py
@@ -17,7 +17,8 @@
 BLK = 128
 NROW = 8
 NCOL = 16
-CHUNK = 10
+CHUNK = 17
+VM = pl.BlockSpec(memory_space=pltpu.VMEM)
 LIFT = 2.0**20
 
 
@@ -329,10 +330,14 @@
     return lax.dot_general(v, linv, (((1,), (1,)), ((), ())), precision=HIGH, preferred_element_type=F32)
 
 
-def last_kernel(rows, cols, linv, out, gram, acc, sib, xbuf, yhbuf, zbuf, ylbuf, mid, s_s, r_s, s_x, r_x, s_z, r_z, s_y, r_y, part, g1, s1, g2, s2, ss, rr):
+def last_kernel(rows, cols, gram_before, out, gram, acc, sib, xbuf, yhbuf, zbuf, ylbuf, mid, s_s, r_s, s_x, r_x, s_z, r_z, s_y, r_y, part, g1, s1, g2, s2, ss, rr, linv):
     w = Where()
     entry_barrier(w.all_group())
-    upper, lower = reduce_scatter(w, rows, cols, acc, sib, xbuf, yhbuf, zbuf, ylbuf, mid, s_s, r_s, s_x, r_x, s_z, r_z, s_y, r_y)
+
+    def between():
+        linv[...] = inverse_factor(gram_before[...].reshape(NV, NV))
+
+    upper, lower = reduce_scatter(w, rows, cols, acc, sib, xbuf, yhbuf, zbuf, ylbuf, mid, s_s, r_s, s_x, r_x, s_z, r_z, s_y, r_y, between)
     out[0] = times_inverse(upper, linv[...])
     out[1] = times_inverse(lower, linv[...])
     part[...] = (self_product(out[0]) + self_product(out[1])).reshape(NCOL, 8, NV)
@@ -344,31 +349,36 @@
 
 
 def inverse_factor(gram):
-    tiles = [gram[t * 8 : t * 8 + 8, :] for t in range(16)]
     lane = lax.broadcasted_iota(jnp.int32, (8, NV), 1)
     sub = lax.broadcasted_iota(jnp.int32, (8, NV), 0)
-    for j in range(NV):
-        t0, i0 = j // 8, j % 8
-        here = lane == j
-        row = tiles[t0][i0 : i0 + 1, :]
-        inv = 1.0 / row[:, j : j + 1]
-        step = jnp.where(here[0:1], 1.0, row) * inv
-        for t in range(t0, 16):
-            tile = tiles[t]
-            col = jnp.broadcast_to(tile[:, j : j + 1], (8, NV))
-            new = jnp.where(here, 0.0, tile) - col * step
-            tiles[t] = jnp.where(sub > i0, new, tile) if t == t0 else new
-    out = []
-    for t in range(16):
-        tile = tiles[t]
-        diag = jnp.sum(jnp.where(lane == sub + 8 * t, tile, 0.0), axis=1, keepdims=True)
-        unit = jnp.where(lane < sub + 8 * t, tile, jnp.where(lane == sub + 8 * t, 1.0, 0.0))
-        out.append(unit * (1.0 / jnp.sqrt(diag)))
-    return jnp.concatenate(out, axis=0)
-
-
-def factor_kernel(gram, linv):
-    linv[...] = inverse_factor(gram[...].reshape(NV, NV))
+    row = lax.broadcasted_iota(jnp.int32, (NV, NV), 0)
+    inside = lax.broadcasted_iota(jnp.int32, (NV, NV), 1) < 8
+    def block(it, w):
+        top = w[:8]
+        cols = [jnp.broadcast_to(w[:, i:i+1], (NV, NV)) for i in range(8)]
+        b = [c[:8] for c in cols]
+        x = jnp.where(lane < 8, jnp.where(lane == sub, 1.0, 0.0), top)
+        fin = x
+        for j in range(8):
+            here = sub == j
+            p = jnp.broadcast_to(b[j][j:j+1], (8, NV))
+            inv = 1.0 / p
+            xr = jnp.broadcast_to(x[j:j+1], (8, NV))
+            fin = jnp.where(here, xr * (1.0 / jnp.sqrt(p)), fin)
+            xs = xr * inv
+            cj = b[j]
+            x = jnp.where(here, xs, x - cj * xs)
+            for k in range(j + 1, 8):
+                bs = jnp.broadcast_to(b[k][j:j+1], (8, NV)) * inv
+                b[k] = jnp.where(here, bs, b[k] - cj * bs)
+        upd = jnp.where(inside, 0.0, w)
+        for i in range(8):
+            upd = upd - cols[i] * jnp.broadcast_to(x[i:i+1], (NV, NV))
+        w = jnp.where(row < NV - 8 * it, upd, w)
+        w = jnp.concatenate([w[8:], fin], axis=0)
+        return pltpu.roll(w, NV - 8, 1)
+    w = lax.fori_loop(0, 16, block, gram)
+    return jnp.where(lax.broadcasted_iota(jnp.int32, (NV, NV), 1) <= row, w, 0.0)
 
 
 def finish_kernel(gram, y, out):
@@ -383,72 +393,81 @@
     return hi, lo
 
 
-def product_kernel(places, blocks, row_side, col_side, rows, cols, wcol, xrow, flipped):
-    step = pl.program_id(0)
-
-    @pl.when(step == 0)
-    def _():
-        @pl.loop(0, 16)
-        def _(i):
-            hi, lo = split(col_side[i])
-            wcol[i] = jnp.concatenate([jnp.concatenate([hi, lo], axis=1)] * 2, axis=0)
-            flipped[i] = jnp.zeros((NV, BLK), F32)
-
-        @pl.loop(0, 32)
-        def _(i):
-            hi, lo = split(row_side[i].T)
-            xrow[i] = jnp.concatenate([hi, lo], axis=1)
-            rows[i] = jnp.zeros((BLK, NV), F32)
-
-    for b in range(CHUNK):
-        k = step * CHUNK + b
-        r = places[0, k]
-        c = places[1, k]
-        hi, lo = split(blocks[b])
-        flat = jnp.concatenate([hi, lo], axis=1)
-        d = jnp.dot(flat, wcol[c], preferred_element_type=F32)
-        rows[r] += d[:, :NV] + d[:, NV:]
-        e = jnp.dot(xrow[r], jnp.concatenate([flat, flat], axis=0), preferred_element_type=F32)
-        flipped[c] += e[:, :BLK] + e[:, BLK:]
-
-    @pl.when(step == pl.num_programs(0) - 1)
-    def _():
-        @pl.loop(0, 16)
-        def _(i):
-            cols[i] = flipped[i].T
+def product_kernel(places, blocks, row_side, col_side, rows, cols, wcol, xrow, flipped, held, sem):
+    listed = blocks.shape[0]
+    steps = listed // CHUNK
+
+    def piece(i):
+        part = pl.ds(i * CHUNK, CHUNK)
+        return pltpu.make_async_copy(blocks.at[part], held.at[part], sem.at[i])
+
+    for i in range(steps):
+        piece(i).start()
+
+    def col_piece(i, carry):
+        hi, lo = split(col_side[i])
+        wcol[i] = jnp.concatenate([jnp.concatenate([hi, lo], axis=1)] * 2, axis=0)
+        flipped[i] = jnp.zeros((NV, BLK), F32)
+        return carry
+
+    def row_piece(i, carry):
+        hi, lo = split(row_side[i].T)
+        xrow[i] = jnp.concatenate([hi, lo], axis=1)
+        rows[i] = jnp.zeros((BLK, NV), F32)
+        return carry
+
+    lax.fori_loop(0, 16, col_piece, 0, unroll=8)
+    lax.fori_loop(0, 32, row_piece, 0, unroll=8)
+
+    def step(i, carry):
+        piece(i).wait()
+        for b in range(CHUNK):
+            k = i * CHUNK + b
+            r = places[0, k]
+            c = places[1, k]
+            hi, lo = split(held[k])
+            flat = jnp.concatenate([hi, lo], axis=1)
+            d = jnp.dot(flat, wcol[c], preferred_element_type=F32)
+            rows[r] += d[:, :NV] + d[:, NV:]
+            e = jnp.dot(xrow[r], jnp.concatenate([flat, flat], axis=0), preferred_element_type=F32)
+            flipped[c] += e[:, :BLK] + e[:, BLK:]
+        return carry
+
+    lax.fori_loop(0, steps, step, 0)
+
+    def back(i, carry):
+        cols[i] = flipped[i].T
+        return carry
+
+    lax.fori_loop(0, 16, back, 0, unroll=8)
 
 
 def products(values, places, rowbuf, colbuf):
     listed = values.shape[0]
-    whole = lambda n: pl.BlockSpec((n, BLK, NV), lambda i, p: (0, 0, 0), pipeline_mode=pl.Buffered(1))
     rows, cols = pl.pallas_call(
         product_kernel,
         out_shape=(
             jax.ShapeDtypeStruct((32, BLK, NV), F32),
             jax.ShapeDtypeStruct((16, BLK, NV), F32),
         ),
-        grid_spec=pltpu.PrefetchScalarGridSpec(
-            num_scalar_prefetch=1,
-            grid=(listed // CHUNK,),
-            in_specs=[
-                pl.BlockSpec((CHUNK, BLK, BLK), lambda i, p: (i, 0, 0)),
-                whole(32),
-                whole(16),
-            ],
-            out_specs=(whole(32), whole(16)),
-            scratch_shapes=[
-                pltpu.VMEM((16, 2 * BLK, 2 * NV), BF16),
-                pltpu.VMEM((32, NV, 2 * BLK), BF16),
-                pltpu.VMEM((16, NV, BLK), F32),
-            ],
-        ),
+        in_specs=[
+            pl.BlockSpec(memory_space=pltpu.SMEM),
+            pl.BlockSpec(memory_space=pl.ANY),
+            VM,
+            VM,
+        ],
+        out_specs=(VM, VM),
+        scratch_shapes=[
+            pltpu.VMEM((16, 2 * BLK, 2 * NV), BF16),
+            pltpu.VMEM((32, NV, 2 * BLK), BF16),
+            pltpu.VMEM((16, NV, BLK), F32),
+            pltpu.VMEM((listed, BLK, BLK), F32),
+            pltpu.SemaphoreType.DMA((listed // CHUNK,)),
+        ],
         compiler_params=pltpu.CompilerParams(vmem_limit_bytes=40 << 20),
         name="tile_products",
     )(places, values, rowbuf.reshape(32, BLK, NV), colbuf.reshape(16, BLK, NV))
     return rows.reshape(NCOL, GROUP, NV), cols.reshape(NROW, GROUP, NV)
-
-
-VM = pl.BlockSpec(memory_space=pltpu.VMEM)
 
 
 def remote_call(kernel, name, cid, ins, outs, scratch):
@@ -481,11 +500,6 @@
         [row_shape, col_shape, gram_shape],
         RS_SCRATCH + [pltpu.VMEM((2, GROUP, NV), F32)] + GATHER_SEMS + GRAM_SCRATCH,
     )(rows, cols)
-    linv = pl.pallas_call(
-        factor_kernel,
-        out_shape=jax.ShapeDtypeStruct((NV, NV), F32),
-        name="factor",
-    )(gram)
     rows, cols = products(values, places, rowbuf, colbuf)
     y, gram = remote_call(
         last_kernel,
@@ -493,8 +507,8 @@
         2,
         3,
         [(2, GROUP, NV), gram_shape],
-        RS_SCRATCH + GRAM_SCRATCH,
-    )(rows, cols, linv)
+        RS_SCRATCH + GRAM_SCRATCH + [pltpu.VMEM((NV, NV), F32)],
+    )(rows, cols, gram)
     return pl.pallas_call(
         finish_kernel,
         out_shape=jax.ShapeDtypeStruct((2, GROUP, NV), F32),

time: 175 us -> 135 us (0.77)
  Pallas kernels: 170 us -> 132 us
    pallas_call x2, Pallas kernels: 41.3 us -> 20 us  [products(): pl.pallas_call(product_kernel, out_shape=(jax.ShapeDtypeStruct((32, BLK,...]
    pallas_call x1 -> x0, Pallas kernels: 12.3 us -> none  [local(): pl.pallas_call(factor_kernel, out_shape=jax.ShapeDtypeStruct((NV, NV), F3...]
    pallas_call x1, Pallas kernels: 12.9 us -> 7.89 us  [local(): pl.pallas_call(finish_kernel, out_shape=jax.ShapeDtypeStruct((2, GROUP, N...]
    unnamed x14 -> x8, local copies, waits for them, and re-layouts: 3.79 us -> 2.93 us
where the time goes in v2:
time: 135 us
  Pallas kernels  132 us (98%)
  local copies, waits for them, and re-layouts  2.93 us (2%)
    pallas_call x1, Pallas kernels, local(): remote_call(middle_kernel, 'middle', 1, 2, [row_shape, col_shape, gram_sh...  43.8 us
    pallas_call x1, Pallas kernels, local(): remote_call(last_kernel, 'last', 2, 3, [(2, GROUP, NV), gram_shape], RS_S...  37.5 us
    pallas_call x1, Pallas kernels, local(): remote_call(gather_kernel, 'gather', 0, 1, [row_shape, col_shape], GATHER...  22.8 us
    pallas_call x2, Pallas kernels, products(): pl.pallas_call(product_kernel, out_shape=(jax.ShapeDtypeStruct((32, BLK,...  20 us
    pallas_call x1, Pallas kernels, local(): pl.pallas_call(finish_kernel, out_shape=jax.ShapeDtypeStruct((2, GROUP, N...  7.89 us
    unnamed x8, local copies, waits for them, and re-layouts  2.93 us

profile of v2, /device:TPU:1, one launch (start us, length us, event | category | flops | bytes accessed | tf_op | source)
XLA Modules:
  0.0 135.0 jit_solution(17615757705572991606)
XLA Ops:
  0.0 0.0 copy-start
  0.0 0.9 copy-done
  1.0 22.8 %gather.1 = (f32[16,256,128]{2,1,0:T(8,128)S(1)}, f32[8,256,128]{2,1,0:T(8,128)S(1)}) custom-call(f32[2,256,128]{2,1,0:T(8,128)S(1)} %copy-done), custom_call_target="tpu_custom_call" | custom-call | tf_op jit(solution)/shard_map/gather/pallas_call | solution.py:493
  23.8 0.0 copy-start.3
  23.8 0.7 copy-done.3
  24.4 9.9 %tile_products.2 = (f32[32,128,128]{2,1,0:T(8,128)S(1)}, f32[16,128,128]{2,1,0:T(8,128)S(1)}) custom-call(s32[2,170]{1,0:T(2,128)S(1)} %bitcast.18, f32[170,128,128]{2,1,0:T(8,128)} %bitcast.20, f32[32,128,128]{2,1,0:T(8,128)S(1)} %bitcast.13, f32[16,128,128]{2,1,0:T(8,128)S(1)} %bitcast.17), custom_call_target="tpu_custom_call" | custom-call | tf_op jit(solution)/shard_map/tile_products/pallas_call | solution.py:447
  34.4 43.8 %middle.1 = (f32[16,256,128]{2,1,0:T(8,128)S(1)}, f32[8,256,128]{2,1,0:T(8,128)S(1)}, f32[16,8,128]{2,1,0:T(8,128)S(1)}) custom-call(f32[16,256,128]{2,1,0:T(8,128)S(1)} %bitcast.10, f32[8,256,128]{2,1,0:T(8,128)S(1)} %bitcast.14), custom_call_target="tpu_custom_call" | custom-call | tf_op jit(solution)/shard_map/middle/pallas_call | solution.py:495
  78.1 10.1 %tile_products.3 = (f32[32,128,128]{2,1,0:T(8,128)S(1)}, f32[16,128,128]{2,1,0:T(8,128)S(1)}) custom-call(s32[2,170]{1,0:T(2,128)S(1)} %bitcast.19, f32[170,128,128]{2,1,0:T(8,128)} %bitcast.21, f32[32,128,128]{2,1,0:T(8,128)S(1)} %bitcast.12, f32[16,128,128]{2,1,0:T(8,128)S(1)} %bitcast.16), custom_call_target="tpu_custom_call" | custom-call | tf_op jit(solution)/shard_map/tile_products/pallas_call | solution.py:447
  88.3 37.5 %last.1 = (f32[2,256,128]{2,1,0:T(8,128)S(1)}, f32[16,8,128]{2,1,0:T(8,128)S(1)}) custom-call(f32[16,256,128]{2,1,0:T(8,128)S(1)} %bitcast.11, f32[8,256,128]{2,1,0:T(8,128)S(1)} %bitcast.15, f32[16,8,128]{2,1,0:T(8,128)S(1)} %get-tuple-element.24.gram_before), custom_call_target="tpu_custom_call" | custom-call | tf_op jit(solution)/shard_map/last/pallas_call | solution.py:504
  125.8 0.0 copy-start.1
  125.8 0.7 copy-done.1
  126.5 0.0 copy-start.2
  126.5 0.6 copy-done.2
  127.1 7.9 %finish.1 = f32[2,256,128]{2,1,0:T(8,128)} custom-call(f32[16,8,128]{2,1,0:T(8,128)} %copy-done.2, f32[2,256,128]{2,1,0:T(8,128)} %copy-done.1), custom_call_target="tpu_custom_call" | custom-call | tf_op jit(solution)/shard_map/finish/pallas_call | solution.py:512
Async XLA Ops:
  0.0 0.9 copy-start
  23.8 0.7 copy-start.3
  125.8 0.7 copy-start.1
  126.5 0.6 copy-start.2

commit v3 on v0

v3 whole, which is shorter than its diff:
```python
import functools

import jax
import jax.numpy as jnp
from jax import lax
from jax.experimental import pallas as pl
from jax.experimental.pallas import tpu as pltpu
from jax.sharding import PartitionSpec as P

MESH = pl.DeviceIdType.MESH
HIGH = lax.Precision.HIGHEST
F32 = jnp.float32
BF16 = jnp.bfloat16

GROUP = 256
NV = 128
BLK = 128
NROW = 8
NCOL = 16
CHUNK = 17
VM = pl.BlockSpec(memory_space=pltpu.VMEM)
LIFT = 2.0**20


class Where:
    def __init__(self):
        self.r = lax.axis_index("row")
        self.c = lax.axis_index("col")
        self.z = self.r // 2
        self.yl = self.r % 2
        self.yh = self.c // 8
        self.x = (self.c // 2) % 4
        self.core = self.c % 2

    def zr(self, dz, other=False):
        yl = 1 - self.yl if other else self.yl
        return ((self.z + dz) % 4) * 2 + yl

    def xc(self, dx, other_y=False, other_core=False):
        yh = 1 - self.yh if other_y else self.yh
        core = 1 - self.core if other_core else self.core
        return (yh * 4 + (self.x + dx) % 4) * 2 + core

    def neighbours(self):
        out = [(self.zr(dz), self.c) for dz in (1, 3)]
        out.append((self.zr(0, True), self.c))
        out += [(self.r, self.xc(dx)) for dx in (1, 3)]
        out.append((self.r, self.xc(0, True)))
        out.append((self.r, self.xc(0, False, True)))
        return out

    def all_group(self):
        out = [((self.r + d) % NROW, self.c) for d in range(1, NROW)]
        out += [(self.r, (self.c + d) % NCOL) for d in range(1, NCOL)]
        return out


def entry_barrier(partners):
    barrier = pltpu.get_barrier_semaphore()
    for p in partners:
        pl.semaphore_signal(barrier, inc=1, device_id=p, device_id_type=MESH)
    pl.semaphore_wait(barrier, len(partners))


def rcopy(src, dst, send, recv, dev):
    return pltpu.make_async_remote_copy(
        src_ref=src,
        dst_ref=dst,
        send_sem=send,
        recv_sem=recv,
        device_id=dev,
        device_id_type=MESH,
    )


HALF = GROUP // 2


def half(ref, h):
    return ref.at[pl.ds(h * HALF, HALF)]


class Posts:
    def __init__(self, pool):
        self.pool = pool
        self.sent = []

    def post(self, src, dst, recv, dev):
        cp = rcopy(src, dst, self.pool.at[len(self.sent)], recv, dev)
        cp.start()
        self.sent.append(cp)
        return cp

    def arrived(self, ref, recv, dev):
        rcopy(ref, ref, self.pool.at[0], recv, dev).wait_recv()

    def drain(self):
        for cp in self.sent:
            cp.wait_send()
        self.sent = []


class Gather:
    def __init__(self, w, posts, up, lo, rowbuf, colbuf, ru, rl):
        self.w, self.posts, self.up, self.lo = w, posts, up, lo
        self.rowbuf, self.colbuf, self.ru, self.rl = rowbuf, colbuf, ru, rl
        self.sibling = (w.r, w.xc(0, False, True))

    def send_u(self, src, p, dev):
        self.posts.post(src, self.rowbuf.at[p], self.ru.at[p], dev)

    def send_l(self, src, q, dev):
        self.posts.post(src, self.colbuf.at[q], self.rl.at[q], dev)

    def wait_u(self, p):
        self.posts.arrived(self.rowbuf.at[p], self.ru.at[p], self.sibling)

    def wait_l(self, q):
        self.posts.arrived(self.colbuf.at[q], self.rl.at[q], self.sibling)

    def start_l(self):
        w = self.w
        self.send_l(self.lo, w.r, (w.zr(0, True), w.c))
        for d in (2, 1, 3):
            self.send_l(self.lo, w.r, (w.zr(d), w.c))
        self.colbuf[w.r] = self.lo[...]

    def start_u(self):
        w = self.w
        self.send_u(self.up, w.c, (w.r, w.xc(0, True)))
        for d in (2, 1, 3):
            self.send_u(self.up, w.c, (w.r, w.xc(d)))
        self.send_u(self.up, w.c, self.sibling)
        self.rowbuf[w.c] = self.up[...]

    def from_y_l(self):
        w = self.w
        q = w.zr(0, True)
        self.wait_l(q)
        for d in (2, 1, 3):
            self.send_l(self.colbuf.at[q], q, (w.zr(d), w.c))

    def from_y_u(self):
        w = self.w
        p = w.xc(0, True)
        self.wait_u(p)
        for d in (2, 1, 3):
            self.send_u(self.rowbuf.at[p], p, (w.r, w.xc(d)))
        self.send_u(self.rowbuf.at[p], p, self.sibling)

    def from_x(self, other):
        for d in (1, 3, 2):
            p = self.w.xc(d, other)
            self.wait_u(p)
            self.send_u(self.rowbuf.at[p], p, self.sibling)

    def rest_l(self):
        for other in (False, True):
            for d in (1, 2, 3):
                self.wait_l(self.w.zr(d, other))

    def rest_u(self):
        for other in (False, True):
            for d in range(4):
                self.wait_u(self.w.xc(d, other, True))


GATHER_SEMS = [pltpu.SemaphoreType.DMA((NCOL,)), pltpu.SemaphoreType.DMA((NROW,))]


class Ring:
    def __init__(self, posts, dev, part, dep, rel, fin, r_rel, r_fin):
        self.posts, self.dev, self.part = posts, dev, part
        self.dep, self.rel, self.fin = dep, rel, fin
        self.r_rel, self.r_fin = r_rel, r_fin

    def far(self, o):
        for k, s in enumerate((1, -1)):
            self.posts.post(half(self.part(2, o), k), self.rel.at[k, o], self.r_rel.at[k, o], self.dev(s))

    def near(self, o):
        for k, s in enumerate((1, -1)):
            h = 1 - k
            self.posts.post(half(self.part(s, o), h), half(self.fin.at[k, o], h), self.r_fin.at[k, o, h], self.dev(s))

    def through(self, o):
        for k, s in enumerate((1, -1)):
            self.posts.arrived(self.rel.at[k, o], self.r_rel.at[k, o], self.dev(s))
            self.dep[k, o] = half(self.part(s, o), k)[...] + self.rel[k, o]
            self.posts.post(self.dep.at[k, o], half(self.fin.at[k, o], k), self.r_fin.at[k, o, k], self.dev(s))

    def total(self, o):
        for k in (0, 1):
            for h in (0, 1):
                self.posts.arrived(half(self.fin.at[k, o], h), self.r_fin.at[k, o, h], self.dev(1))
        return self.part(0, o)[...] + self.fin[0, o] + self.fin[1, o]


def reduce_scatter(w, posts, rows, cols, scratch, flip, on_lower, on_upper, beside):
    acc, sib, r_sib, depx, relx, finx, r_relx, r_finx, depz, relz, finz, r_relz, r_finz, mid, ybuf, r_y = scratch
    sibling = (w.r, w.xc(0, False, True))
    slots = [(2, 1), (1, 1), (3, 1), (2, 0), (1, 0), (3, 0), (0, 1), (0, 0)]
    at = {s: i for i, s in enumerate(slots)}

    def xpart(d, o):
        return acc.at[at[d % 4, o]]

    def zpart(d, o):
        return cols.at[w.zr(d % 4, o == 1)]

    xr = Ring(posts, lambda s: (w.r, w.xc(s % 4)), xpart, depx, relx, finx, r_relx, r_finx)
    zr = Ring(posts, lambda s: (w.zr(s % 4), w.c), zpart, depz, relz, finz, r_relz, r_finz)

    def join(*ids):
        for i in ids:
            posts.arrived(sib.at[i], r_sib.at[i], sibling)
            d, o = slots[i]
            acc[i] = rows[w.xc(d, o == 1)] + sib[i]

    for i, (d, o) in enumerate(slots):
        posts.post(rows.at[w.xc(d, o == 1, True)], sib.at[i], r_sib.at[i], sibling)
    flip(0)
    join(0)
    xr.far(1)
    join(1, 2)
    xr.near(1)
    join(3)
    xr.far(0)
    join(4, 5)
    flip(1)
    zr.far(1)
    zr.near(1)
    zr.far(0)
    xr.through(1)
    xr.near(0)
    zr.near(0)
    join(6, 7)
    xr.through(0)
    beside(0)
    zr.through(1)
    zr.through(0)
    beside(1)
    mid[1] = xr.total(1)
    for h in (0, 1):
        posts.post(half(mid.at[1], h), half(ybuf.at[1], h), r_y.at[1, h], (w.r, w.xc(0, True)))
    beside(2)
    mid[0] = zr.total(1)
    for h in (0, 1):
        posts.post(half(mid.at[0], h), half(ybuf.at[0], h), r_y.at[0, h], (w.zr(0, True), w.c))
    mid[3] = xr.total(0)
    beside(3)
    for h in (0, 1):
        posts.arrived(half(ybuf.at[1], h), r_y.at[1, h], sibling)
    on_upper(mid[3] + ybuf[1])
    mid[2] = zr.total(0)
    for h in (0, 1):
        posts.arrived(half(ybuf.at[0], h), r_y.at[0, h], sibling)
    on_lower(mid[2] + ybuf[0])


RING_SCRATCH = [
    pltpu.VMEM((2, 2, HALF, NV), F32),
    pltpu.VMEM((2, 2, HALF, NV), F32),
    pltpu.VMEM((2, 2, GROUP, NV), F32),
    pltpu.SemaphoreType.DMA((2, 2)),
    pltpu.SemaphoreType.DMA((2, 2, 2)),
]
RS_SCRATCH = (
    [
        pltpu.VMEM((8, GROUP, NV), F32),
        pltpu.VMEM((8, GROUP, NV), F32),
        pltpu.SemaphoreType.DMA((8,)),
    ]
    + RING_SCRATCH
    + RING_SCRATCH
    + [
        pltpu.VMEM((4, GROUP, NV), F32),
        pltpu.VMEM((2, GROUP, NV), F32),
        pltpu.SemaphoreType.DMA((2, 2)),
    ]
)
POOL = pltpu.SemaphoreType.DMA((128,))


class GramSum:
    def __init__(self, w, posts, full, part, g1, s1, g2, s2, rr):
        self.w, self.posts, self.full = w, posts, full
        self.part, self.g1, self.s1, self.g2, self.s2, self.rr = part, g1, s1, g2, s2, rr

    def over_col(self, lo, src, dst):
        w = self.w
        self.cps = []
        for d in range(1, NCOL):
            to = (w.c + d) % NCOL
            self.cps.append(self.posts.post(src(to), dst.at[w.c], self.rr.at[lo + d], (w.r, to)))

    def join(self):
        for cp in self.cps:
            cp.wait_recv()

    def phase1(self):
        w = self.w
        self.over_col(0, lambda to: self.part.at[to], self.g1)
        self.g1[w.c] = self.part[w.c]

    def phase2(self):
        w = self.w
        self.join()
        total = self.g1[0]
        for i in range(1, NCOL):
            total = total + self.g1[i]
        self.s1[...] = total
        self.cps = []
        for d in range(1, NROW):
            to = ((w.r + d) % NROW, w.c)
            self.cps.append(self.posts.post(self.s1, self.g2.at[w.r], self.rr.at[NCOL + d], to))
        self.g2[w.r] = total

    def phase3(self):
        w = self.w
        self.join()
        total = self.g2[0]
        for i in range(1, NROW):
            total = total + self.g2[i]
        total = total * (1.0 / (2 * GROUP * NROW * NCOL))
        self.s2[...] = total
        self.over_col(NCOL + NROW, lambda to: self.s2, self.full)
        self.full[w.c] = total


GRAM_SCRATCH = [
    pltpu.VMEM((NCOL, 8, NV), F32),
    pltpu.VMEM((NCOL, 8, NV), F32),
    pltpu.VMEM((8, NV), F32),
    pltpu.VMEM((NROW, 8, NV), F32),
    pltpu.VMEM((8, NV), F32),
    pltpu.SemaphoreType.DMA((2 * NCOL + NROW,)),
]
NG = len(GRAM_SCRATCH)
NR = len(RS_SCRATCH)


def self_product(v):
    return lax.dot_general(v, v, (((0,), (0,)), ((), ())), precision=HIGH, preferred_element_type=F32)


def times_inverse(v, linv):
    return lax.dot_general(v, linv, (((1,), (1,)), ((), ())), precision=HIGH, preferred_element_type=F32)


def eliminate(gram, first, last):
    lane = lax.broadcasted_iota(jnp.int32, (8, NV), 1)
    sub = lax.broadcasted_iota(jnp.int32, (8, NV), 0)
    row = lax.broadcasted_iota(jnp.int32, (NV, NV), 0)
    inside = lax.broadcasted_iota(jnp.int32, (NV, NV), 1) < 8
    def block(it, w):
        top = w[:8]
        cols = [jnp.broadcast_to(w[:, i:i+1], (NV, NV)) for i in range(8)]
        b = [c[:8] for c in cols]
        x = jnp.where(lane < 8, jnp.where(lane == sub, 1.0, 0.0), top)
        fin = x
        for j in range(8):
            here = sub == j
            p = jnp.broadcast_to(b[j][j:j+1], (8, NV))
            inv = 1.0 / p
            xr = jnp.broadcast_to(x[j:j+1], (8, NV))
            fin = jnp.where(here, xr * (1.0 / jnp.sqrt(p)), fin)
            xs = xr * inv
            cj = b[j]
            x = jnp.where(here, xs, x - cj * xs)
            for k in range(j + 1, 8):
                bs = jnp.broadcast_to(b[k][j:j+1], (8, NV)) * inv
                b[k] = jnp.where(here, bs, b[k] - cj * bs)
        upd = jnp.where(inside, 0.0, w)
        for i in range(8):
            upd = upd - cols[i] * jnp.broadcast_to(x[i:i+1], (NV, NV))
        w = jnp.where(row < NV - 8 * it, upd, w)
        w = jnp.concatenate([w[8:], fin], axis=0)
        return pltpu.roll(w, NV - 8, 1)
    return lax.fori_loop(first, last, block, gram)


def lower_part(w):
    row = lax.broadcasted_iota(jnp.int32, (NV, NV), 0)
    return jnp.where(lax.broadcasted_iota(jnp.int32, (NV, NV), 1) <= row, w, 0.0)


def split(v):
    hi = v.astype(BF16)
    lo = (v - hi.astype(F32)).astype(BF16)
    return hi, lo


def link_kernel(places, links, ends, last_row, last_col):
    listed = places.shape[1]
    for i in range(32):
        last_row[i] = 0
    for i in range(16):
        last_col[i] = 0
    for k in range(listed):
        r = places[0, k]
        c = places[1, k]
        links[0, k] = last_row[r]
        links[1, k] = last_col[c]
        last_row[r] = k + 1
        last_col[c] = k + 1
    for i in range(32):
        ends[0, i] = last_row[i]
    for i in range(16):
        ends[1, i] = last_col[i]


class Tile:
    def __init__(self, places, links, ends, blocks, sem, flat, chain, wcol, xrow):
        self.places, self.links, self.ends, self.blocks, self.sem = places, links, ends, blocks, sem
        self.flat, self.chain, self.wcol, self.xrow = flat, chain, wcol, xrow
        self.steps = blocks.shape[0] // CHUNK

    def piece(self, i):
        return pltpu.make_async_copy(
            self.blocks.at[pl.ds(i * CHUNK, CHUNK)],
            self.chain.at[pl.ds(i * CHUNK + 1, CHUNK)],
            self.sem.at[i],
        )

    def fetch(self):
        for i in range(self.steps):
            self.piece(i).start()

    def convert(self, lo, hi):
        for i in range(lo, hi):
            self.piece(i).wait()

            def one(k, carry):
                hi_part, lo_part = split(self.chain[i * CHUNK + 1 + k])
                self.flat[i * CHUNK + k] = jnp.concatenate([hi_part, lo_part], axis=1)
                return carry

            lax.fori_loop(0, CHUNK, one, 0, unroll=CHUNK)

    def clear(self):
        self.chain[0] = jnp.zeros((BLK, BLK), F32)

    def take_cols(self, colbuf):
        def one(i, carry):
            hi, lo = split(colbuf[i])
            for h in (0, 1):
                a, b = hi[h * BLK : (h + 1) * BLK], lo[h * BLK : (h + 1) * BLK]
                self.wcol[2 * i + h] = jnp.concatenate([jnp.concatenate([a, b], axis=1)] * 2, axis=0)
            return carry

        lax.fori_loop(0, NROW, one, 0, unroll=4)

    def take_rows(self, rowbuf):
        def one(i, carry):
            hi, lo = split(rowbuf[i].T)
            for h in (0, 1):
                a, b = hi[:, h * BLK : (h + 1) * BLK], lo[:, h * BLK : (h + 1) * BLK]
                self.xrow[2 * i + h] = jnp.concatenate([a, b], axis=1)
            return carry

        lax.fori_loop(0, NCOL, one, 0, unroll=4)

    def direct(self, rows):
        def step(i, carry):
            for b in range(CHUNK):
                k = i * CHUNK + b
                d = jnp.dot(self.flat[k], self.wcol[self.places[1, k]], preferred_element_type=F32)
                self.chain[k + 1] = d[:, :NV] + d[:, NV:] + self.chain[self.links[0, k]]
            return carry

        lax.fori_loop(0, self.steps, step, 0)

        def out(i, carry):
            for h in (0, 1):
                rows[i, pl.ds(h * BLK, BLK)] = self.chain[self.ends[0, 2 * i + h]]
            return carry

        lax.fori_loop(0, NCOL, out, 0, unroll=4)

    def flip(self, lo, hi):
        def step(i, carry):
            for b in range(CHUNK):
                k = i * CHUNK + b
                flat = self.flat[k]
                e = jnp.dot(
                    self.xrow[self.places[0, k]],
                    jnp.concatenate([flat, flat], axis=0),
                    preferred_element_type=F32,
                )
                self.chain[k + 1] = e[:, :BLK] + e[:, BLK:] + self.chain[self.links[1, k]]
            return carry

        lax.fori_loop(lo, hi, step, 0)

    def flipped(self, cols):
        def out(i, carry):
            for h in (0, 1):
                cols[i, pl.ds(h * BLK, BLK)] = self.chain[self.ends[1, 2 * i + h]].T
            return carry

        lax.fori_loop(0, NROW, out, 0, unroll=4)


APP_SCRATCH = (
    [pltpu.VMEM((NCOL, GROUP, NV), F32), pltpu.VMEM((NROW, GROUP, NV), F32)]
    + GATHER_SEMS
    + RS_SCRATCH
    + [pltpu.VMEM((NCOL, 8, NV), F32)]
    + GRAM_SCRATCH
)
NA = len(APP_SCRATCH)


def whole_kernel(places, links, ends, blocks, vec, out, sem, flat, chain, wcol, xrow, rows, cols, pool, work, *scratch):
    w = Where()
    tile = Tile(places, links, ends, blocks, sem, flat, chain, wcol, xrow)
    tile.fetch()
    entry_barrier(w.all_group())
    posts = Posts(pool)

    class App:
        def __init__(self, refs, up, lo):
            self.rowbuf, self.colbuf, ru, rl = refs[:4]
            self.rs = refs[4 : 4 + NR]
            self.full = refs[4 + NR]
            self.gram = GramSum(w, posts, self.full, *refs[5 + NR :])
            self.part = refs[5 + NR]
            self.g = Gather(w, posts, up, lo, self.rowbuf, self.colbuf, ru, rl)

        def apply(self, on_lower, on_upper, beside):
            self.g.rest_l()
            tile.take_cols(self.colbuf)
            tile.direct(rows)

            def flip(i):
                if i == 0:
                    self.g.rest_u()
                    tile.take_rows(self.rowbuf)
                    tile.flip(0, tile.steps // 2)
                else:
                    tile.flip(tile.steps // 2, tile.steps)
                    tile.flipped(cols)

            reduce_scatter(w, posts, rows, cols, self.rs, flip, on_lower, on_upper, beside)

        def product(self, y):
            self.part[...] = (self_product(y[0]) + self_product(y[1])).reshape(NCOL, 8, NV)

    one = App(scratch[:NA], vec.at[0], vec.at[1])
    two = App(scratch[NA : 2 * NA], out.at[0], out.at[1])
    third = tile.steps // 3
    one.g.start_l()
    one.g.start_u()
    tile.clear()
    tile.convert(0, third)
    one.g.from_y_l()
    one.g.from_y_u()
    tile.convert(third, 2 * third)
    one.g.from_x(False)
    tile.convert(2 * third, tile.steps)
    one.g.from_x(True)

    def lower_one(v):
        out[1] = v * LIFT
        two.g.start_l()

    def upper_one(v):
        out[0] = v * LIFT
        two.g.start_u()

    one.apply(lower_one, upper_one, lambda i: None)
    one.product(out)
    one.gram.phase1()
    two.g.from_y_u()
    two.g.from_y_l()
    one.gram.phase2()
    two.g.from_x(False)
    one.gram.phase3()
    two.g.from_x(True)
    one.gram.join()
    posts.drain()

    def beside(i):
        state = one.full[...].reshape(NV, NV) if i == 0 else work[...]
        work[...] = eliminate(state, 4 * i, 4 * i + 4)

    def lower_two(v):
        out[1] = times_inverse(v, lower_part(work[...]))

    def upper_two(v):
        out[0] = times_inverse(v, lower_part(work[...]))

    two.apply(lower_two, upper_two, beside)
    two.product(out)
    two.gram.phase1()
    two.gram.phase2()
    two.gram.phase3()
    two.gram.join()
    linv = lower_part(eliminate(two.full[...].reshape(NV, NV), 0, 16))
    posts.drain()
    out[0] = times_inverse(out[0], linv)
    out[1] = times_inverse(out[1], linv)


def local(blocks, coords, vectors):
    values = blocks.reshape(blocks.shape[2], BLK, BLK)
    places = coords.reshape(2, coords.shape[3])
    listed = values.shape[0]
    scalars = pl.BlockSpec(memory_space=pltpu.SMEM)
    links, ends = pl.pallas_call(
        link_kernel,
        out_shape=(
            jax.ShapeDtypeStruct((2, listed), jnp.int32),
            jax.ShapeDtypeStruct((2, 32), jnp.int32),
        ),
        in_specs=[scalars],
        out_specs=(scalars, scalars),
        scratch_shapes=[pltpu.SMEM((32,), jnp.int32), pltpu.SMEM((16,), jnp.int32)],
        name="links",
    )(places)
    return pl.pallas_call(
        whole_kernel,
        out_shape=jax.ShapeDtypeStruct((2, GROUP, NV), F32),
        in_specs=[scalars] * 3 + [pl.BlockSpec(memory_space=pl.ANY), VM],
        out_specs=VM,
        scratch_shapes=[
            pltpu.SemaphoreType.DMA((listed // CHUNK,)),
            pltpu.VMEM((listed, BLK, 2 * BLK), BF16),
            pltpu.VMEM((listed + 1, BLK, BLK), F32),
            pltpu.VMEM((16, 2 * BLK, 2 * NV), BF16),
            pltpu.VMEM((32, NV, 2 * BLK), BF16),
            pltpu.VMEM((NCOL, GROUP, NV), F32),
            pltpu.VMEM((NROW, GROUP, NV), F32),
            POOL,
            pltpu.VMEM((NV, NV), F32),
        ]
        + APP_SCRATCH
        + APP_SCRATCH,
        compiler_params=pltpu.CompilerParams(
            collective_id=0, has_side_effects=True, vmem_limit_bytes=56 << 20
        ),
        name="whole",
    )(places, links, ends, values, vectors)


def solution(mesh):
    return jax.shard_map(
        local,
        mesh=mesh,
        in_specs=(
            P("row", "col", None, None, None),
            P("row", "col", None, None),
            P(None, ("row", "col"), None),
        ),
        out_specs=P(None, ("row", "col"), None),
        check_vma=False,
    )
```

time: 855 us -> 125 us (0.15); the launches traced: 846 us -> 125 us
  waiting for transfers between devices: 437 us -> 0 us
  local copies, waits for them, and re-layouts: 210 us -> 1.67 us
  matrix products: 135 us -> 0 us
  Pallas kernels: 0 us -> 123 us
  other arithmetic: 49.9 us -> 0 us
  between operations: 14 us -> 0.02 us
    psum x2 -> x0, waiting for transfers between devices: 289 us -> none  [local(): gram_sum = lax.psum(partial_gram, ('row', 'col')) / total_rows]
    dot_general x12 -> x0, matrix products: 128 us -> none  [the longest x2 46.9 us: tile_products(): jnp.einsum('kab,kbv->kav', values, col_pieces, precision=exact_mode)]
    pallas_call x0 -> x2, Pallas kernels: none -> 123 us  [the longest x1 121 us: local(): pl.pallas_call(whole_kernel, out_shape=jax.ShapeDtypeStruct((2, GROUP, NV...]
    unnamed x8 -> x1, local copies, waits for them, and re-layouts: 115 us -> 1.67 us
    reduce_scatter x4 -> x0, waiting for transfers between devices: 78.6 us -> none  [the longest x2 78.5 us: local(): lax.psum_scatter(out_cols, 'row', scatter_dimension=0, tiled=True)]
    all_gather x4 -> x0, waiting for transfers between devices: 68.6 us -> none  [the longest x2 68.6 us: local(): col_side = lax.all_gather(current[1], 'row', axis=0, tiled=True)]
    dot_general x4 -> x0, local copies, waits for them, and re-layouts: 48.3 us -> none  [the longest x2 24.3 us: tile_products(): jnp.einsum('kab,kbv->kav', values, col_pieces, precision=exact_mode)]
    another operation x11 -> x0, other arithmetic: 45.7 us -> none  [the longest x6 24.8 us: local(): factor = jnp.linalg.cholesky(gram_sum)]
  transfers between devices with their start and end apart: 10 -> 0, of which waited for: 6 -> 0; matrix products, arithmetic and copies ran while one was open for 40% -> 0% of each run, Pallas kernels for 0% -> 0%
where the time goes in v3:
time: 125 us
  Pallas kernels  123 us (98%)
  local copies, waits for them, and re-layouts  1.67 us (1%)
    pallas_call x1, Pallas kernels, local(): pl.pallas_call(whole_kernel, out_shape=jax.ShapeDtypeStruct((2, GROUP, NV...  121 us

profile of v3, /device:TPU:1, one launch (start us, length us, event | category | flops | bytes accessed | tf_op | source)
XLA Modules:
  0.0 124.9 jit_solution(11632406241583160085)
XLA Ops:
  0.0 1.9 %links.1 = (s32[2,170]{1,0:T(2,128)}, s32[2,32]{1,0:T(2,128)}) custom-call(s32[2,170]{1,0:T(2,128)} %bitcast.3), custom_call_target="tpu_custom_call" | custom-call | tf_op jit(solution)/shard_map/links/pallas_call | solution.py:611
  1.9 121.4 %whole.1 = f32[2,256,128]{2,1,0:T(8,128)} custom-call(s32[2,170]{1,0:T(2,128)} %bitcast.4, s32[2,170]{1,0:T(2,128)} %get-tuple-element.7.links, s32[2,32]{1,0:T(2,128)} %get-tuple-element.8.ends, f32[170,128,128]{2,1,0:T(8,128)} %bitcast.2, f32[2,256,128]{2,1,0:T(8,128)} %vec.1), custom_call_target="tpu_custom_call" | custom-call | tf_op jit(solution)/shard_map/whole/pallas_call | solution.py:622
  123.3 1.7 %copy.5 = f32[2,256,128]{2,1,0:T(8,128)} copy(f32[2,256,128]{2,1,0:T(8,128)} %whole.1) | data formatting | bytes 524288

commit v4 on v3

--- a/solution.py
+++ b/solution.py
@@ -42,16 +42,11 @@
         return (yh * 4 + (self.x + dx) % 4) * 2 + core
 
     def neighbours(self):
-        out = [(self.zr(dz), self.c) for dz in (1, 3)]
+        out = [(self.zr(dz), self.c) for dz in (1, 2, 3)]
         out.append((self.zr(0, True), self.c))
-        out += [(self.r, self.xc(dx)) for dx in (1, 3)]
+        out += [(self.r, self.xc(dx)) for dx in (1, 2, 3)]
         out.append((self.r, self.xc(0, True)))
         out.append((self.r, self.xc(0, False, True)))
-        return out
-
-    def all_group(self):
-        out = [((self.r + d) % NROW, self.c) for d in range(1, NROW)]
-        out += [(self.r, (self.c + d) % NCOL) for d in range(1, NCOL)]
         return out
 
 
@@ -84,9 +79,14 @@
     def __init__(self, pool):
         self.pool = pool
         self.sent = []
+        self.oldest = 0
 
     def post(self, src, dst, recv, dev):
-        cp = rcopy(src, dst, self.pool.at[len(self.sent)], recv, dev)
+        slots = self.pool.shape[0]
+        if len(self.sent) - self.oldest == slots:
+            self.sent[self.oldest].wait_send()
+            self.oldest += 1
+        cp = rcopy(src, dst, self.pool.at[len(self.sent) % slots], recv, dev)
         cp.start()
         self.sent.append(cp)
         return cp
@@ -95,50 +95,55 @@
         rcopy(ref, ref, self.pool.at[0], recv, dev).wait_recv()
 
     def drain(self):
-        for cp in self.sent:
+        for cp in self.sent[self.oldest :]:
             cp.wait_send()
-        self.sent = []
+        self.oldest = len(self.sent)
 
 
 class Gather:
-    def __init__(self, w, posts, up, lo, rowbuf, colbuf, ru, rl):
+    def __init__(self, w, posts, up, lo, rowbuf, colbuf, r_u, r_sib, r_y, r_l):
         self.w, self.posts, self.up, self.lo = w, posts, up, lo
-        self.rowbuf, self.colbuf, self.ru, self.rl = rowbuf, colbuf, ru, rl
+        self.rowbuf, self.colbuf = rowbuf, colbuf
+        self.r_u, self.r_sib, self.r_y, self.r_l = r_u, r_sib.at[0], r_y.at[0], r_l.at[0]
         self.sibling = (w.r, w.xc(0, False, True))
 
     def send_u(self, src, p, dev):
-        self.posts.post(src, self.rowbuf.at[p], self.ru.at[p], dev)
-
-    def send_l(self, src, q, dev):
-        self.posts.post(src, self.colbuf.at[q], self.rl.at[q], dev)
+        self.posts.post(src, self.rowbuf.at[p], self.r_u.at[p // 2], dev)
+
+    def to_sibling(self, src, p):
+        self.posts.post(src, self.rowbuf.at[p], self.r_sib, self.sibling)
+
+    def send_l(self, src, q, recv, dev):
+        self.posts.post(src, self.colbuf.at[q], recv, dev)
 
     def wait_u(self, p):
-        self.posts.arrived(self.rowbuf.at[p], self.ru.at[p], self.sibling)
-
-    def wait_l(self, q):
-        self.posts.arrived(self.colbuf.at[q], self.rl.at[q], self.sibling)
+        self.posts.arrived(self.rowbuf.at[p], self.r_u.at[p // 2], self.sibling)
+
+    def start_y_l(self):
+        self.send_l(self.lo, self.w.r, self.r_y, (self.w.zr(0, True), self.w.c))
+
+    def start_y_u(self):
+        self.send_u(self.up, self.w.c, (self.w.r, self.w.xc(0, True)))
 
     def start_l(self):
         w = self.w
-        self.send_l(self.lo, w.r, (w.zr(0, True), w.c))
         for d in (2, 1, 3):
-            self.send_l(self.lo, w.r, (w.zr(d), w.c))
+            self.send_l(self.lo, w.r, self.r_l, (w.zr(d), w.c))
         self.colbuf[w.r] = self.lo[...]
 
     def start_u(self):
         w = self.w
-        self.send_u(self.up, w.c, (w.r, w.xc(0, True)))
         for d in (2, 1, 3):
             self.send_u(self.up, w.c, (w.r, w.xc(d)))
-        self.send_u(self.up, w.c, self.sibling)
+        self.to_sibling(self.up, w.c)
         self.rowbuf[w.c] = self.up[...]
 
     def from_y_l(self):
         w = self.w
         q = w.zr(0, True)
-        self.wait_l(q)
+        self.posts.arrived(self.colbuf.at[q], self.r_y, self.sibling)
         for d in (2, 1, 3):
-            self.send_l(self.colbuf.at[q], q, (w.zr(d), w.c))
+            self.send_l(self.colbuf.at[q], q, self.r_l, (w.zr(d), w.c))
 
     def from_y_u(self):
         w = self.w
@@ -146,26 +151,23 @@
         self.wait_u(p)
         for d in (2, 1, 3):
             self.send_u(self.rowbuf.at[p], p, (w.r, w.xc(d)))
-        self.send_u(self.rowbuf.at[p], p, self.sibling)
-
-    def from_x(self, other):
-        for d in (1, 3, 2):
+        self.to_sibling(self.rowbuf.at[p], p)
+
+    def from_x(self, other, steps=(1, 3, 2)):
+        for d in steps:
             p = self.w.xc(d, other)
             self.wait_u(p)
-            self.send_u(self.rowbuf.at[p], p, self.sibling)
+            self.to_sibling(self.rowbuf.at[p], p)
 
     def rest_l(self):
-        for other in (False, True):
-            for d in (1, 2, 3):
-                self.wait_l(self.w.zr(d, other))
+        self.posts.arrived(self.colbuf.at[pl.ds(0, 6)], self.r_l, self.sibling)
 
     def rest_u(self):
-        for other in (False, True):
-            for d in range(4):
-                self.wait_u(self.w.xc(d, other, True))
-
-
-GATHER_SEMS = [pltpu.SemaphoreType.DMA((NCOL,)), pltpu.SemaphoreType.DMA((NROW,))]
+        self.posts.arrived(self.rowbuf.at[pl.ds(0, 8)], self.r_sib, self.sibling)
+
+
+GATHER_SEMS = [pltpu.SemaphoreType.DMA((n,)) for n in (8, 1, 1, 1)]
+NS = len(GATHER_SEMS)
 
 
 class Ring:
@@ -176,94 +178,85 @@
 
     def far(self, o):
         for k, s in enumerate((1, -1)):
-            self.posts.post(half(self.part(2, o), k), self.rel.at[k, o], self.r_rel.at[k, o], self.dev(s))
+            self.posts.post(half(self.part(2, o), k), self.rel.at[o, k], self.r_rel.at[o], self.dev(s))
 
     def near(self, o):
         for k, s in enumerate((1, -1)):
             h = 1 - k
-            self.posts.post(half(self.part(s, o), h), half(self.fin.at[k, o], h), self.r_fin.at[k, o, h], self.dev(s))
+            self.posts.post(half(self.part(s, o), h), half(self.fin.at[o, k], h), self.r_fin.at[o], self.dev(s))
 
     def through(self, o):
+        self.posts.arrived(self.rel.at[o], self.r_rel.at[o], self.dev(1))
         for k, s in enumerate((1, -1)):
-            self.posts.arrived(self.rel.at[k, o], self.r_rel.at[k, o], self.dev(s))
-            self.dep[k, o] = half(self.part(s, o), k)[...] + self.rel[k, o]
-            self.posts.post(self.dep.at[k, o], half(self.fin.at[k, o], k), self.r_fin.at[k, o, k], self.dev(s))
+            self.dep[o, k] = half(self.part(s, o), k)[...] + self.rel[o, k]
+            self.posts.post(self.dep.at[o, k], half(self.fin.at[o, k], k), self.r_fin.at[o], self.dev(s))
 
     def total(self, o):
-        for k in (0, 1):
-            for h in (0, 1):
-                self.posts.arrived(half(self.fin.at[k, o], h), self.r_fin.at[k, o, h], self.dev(1))
-        return self.part(0, o)[...] + self.fin[0, o] + self.fin[1, o]
-
-
-def reduce_scatter(w, posts, rows, cols, scratch, flip, on_lower, on_upper, beside):
-    acc, sib, r_sib, depx, relx, finx, r_relx, r_finx, depz, relz, finz, r_relz, r_finz, mid, ybuf, r_y = scratch
-    sibling = (w.r, w.xc(0, False, True))
-    slots = [(2, 1), (1, 1), (3, 1), (2, 0), (1, 0), (3, 0), (0, 1), (0, 0)]
-    at = {s: i for i, s in enumerate(slots)}
-
-    def xpart(d, o):
-        return acc.at[at[d % 4, o]]
-
-    def zpart(d, o):
-        return cols.at[w.zr(d % 4, o == 1)]
-
-    xr = Ring(posts, lambda s: (w.r, w.xc(s % 4)), xpart, depx, relx, finx, r_relx, r_finx)
-    zr = Ring(posts, lambda s: (w.zr(s % 4), w.c), zpart, depz, relz, finz, r_relz, r_finz)
-
-    def join(*ids):
+        self.posts.arrived(self.fin.at[o], self.r_fin.at[o], self.dev(1))
+        return self.part(0, o)[...] + self.fin[o, 0] + self.fin[o, 1]
+
+
+class Scatter:
+    SLOTS = [(2, 1), (1, 1), (3, 1), (2, 0), (1, 0), (3, 0), (0, 1), (0, 0)]
+
+    def __init__(self, w, posts, rows, cols, scratch):
+        self.acc, self.sib, self.r_sib = scratch[:3]
+        x, z = scratch[3:8], scratch[8:13]
+        self.mid, self.ybuf, self.r_y = scratch[13:]
+        self.w, self.posts, self.rows = w, posts, rows
+        self.sibling = (w.r, w.xc(0, False, True))
+        at = {slot: i for i, slot in enumerate(self.SLOTS)}
+        self.x = Ring(posts, lambda s: (w.r, w.xc(s % 4)), lambda d, o: self.acc.at[at[d % 4, o]], *x)
+        self.z = Ring(posts, lambda s: (w.zr(s % 4), w.c), lambda d, o: cols.at[w.zr(d % 4, o == 1)], *z)
+
+    def siblings(self):
+        for i, (d, o) in enumerate(self.SLOTS):
+            src = self.rows.at[self.w.xc(d, o == 1, True)]
+            self.posts.post(src, self.sib.at[i], self.r_sib.at[i], self.sibling)
+
+    def join(self, *ids):
         for i in ids:
-            posts.arrived(sib.at[i], r_sib.at[i], sibling)
-            d, o = slots[i]
-            acc[i] = rows[w.xc(d, o == 1)] + sib[i]
-
-    for i, (d, o) in enumerate(slots):
-        posts.post(rows.at[w.xc(d, o == 1, True)], sib.at[i], r_sib.at[i], sibling)
-    flip(0)
-    join(0)
-    xr.far(1)
-    join(1, 2)
-    xr.near(1)
-    join(3)
-    xr.far(0)
-    join(4, 5)
-    flip(1)
-    zr.far(1)
-    zr.near(1)
-    zr.far(0)
-    xr.through(1)
-    xr.near(0)
-    zr.near(0)
-    join(6, 7)
-    xr.through(0)
-    beside(0)
-    zr.through(1)
-    zr.through(0)
-    beside(1)
-    mid[1] = xr.total(1)
-    for h in (0, 1):
-        posts.post(half(mid.at[1], h), half(ybuf.at[1], h), r_y.at[1, h], (w.r, w.xc(0, True)))
-    beside(2)
-    mid[0] = zr.total(1)
-    for h in (0, 1):
-        posts.post(half(mid.at[0], h), half(ybuf.at[0], h), r_y.at[0, h], (w.zr(0, True), w.c))
-    mid[3] = xr.total(0)
-    beside(3)
-    for h in (0, 1):
-        posts.arrived(half(ybuf.at[1], h), r_y.at[1, h], sibling)
-    on_upper(mid[3] + ybuf[1])
-    mid[2] = zr.total(0)
-    for h in (0, 1):
-        posts.arrived(half(ybuf.at[0], h), r_y.at[0, h], sibling)
-    on_lower(mid[2] + ybuf[0])
+            self.posts.arrived(self.sib.at[i], self.r_sib.at[i], self.sibling)
+            d, o = self.SLOTS[i]
+            self.acc[i] = self.rows[self.w.xc(d, o == 1)] + self.sib[i]
+
+    def far_x(self):
+        self.join(0)
+        self.x.far(1)
+        self.join(1, 2)
+        self.x.near(1)
+        self.join(3)
+        self.x.far(0)
+
+    def far_z(self):
+        self.z.far(1)
+        self.z.near(1)
+        self.z.far(0)
+
+    def to_y(self, j, dev, value):
+        self.mid[j] = value
+        self.posts.post(self.mid.at[j], self.ybuf.at[j], self.r_y.at[j], dev)
+
+    def to_y_x(self):
+        self.to_y(1, (self.w.r, self.w.xc(0, True)), self.x.total(1))
+
+    def to_y_z(self):
+        self.to_y(0, (self.w.zr(0, True), self.w.c), self.z.total(1))
+
+    def own(self, j, ring):
+        self.mid[2 + j] = ring.total(0)
+
+    def final(self, j):
+        self.posts.arrived(self.ybuf.at[j], self.r_y.at[j], self.sibling)
+        return self.mid[2 + j] + self.ybuf[j]
 
 
 RING_SCRATCH = [
     pltpu.VMEM((2, 2, HALF, NV), F32),
     pltpu.VMEM((2, 2, HALF, NV), F32),
     pltpu.VMEM((2, 2, GROUP, NV), F32),
-    pltpu.SemaphoreType.DMA((2, 2)),
-    pltpu.SemaphoreType.DMA((2, 2, 2)),
+    pltpu.SemaphoreType.DMA((2,)),
+    pltpu.SemaphoreType.DMA((2,)),
 ]
 RS_SCRATCH = (
     [
@@ -276,27 +269,33 @@
     + [
         pltpu.VMEM((4, GROUP, NV), F32),
         pltpu.VMEM((2, GROUP, NV), F32),
-        pltpu.SemaphoreType.DMA((2, 2)),
+        pltpu.SemaphoreType.DMA((2,)),
     ]
 )
-POOL = pltpu.SemaphoreType.DMA((128,))
+POOLS = [pltpu.SemaphoreType.DMA((n,)) for n in (34, 22, 34)]
 
 
 class GramSum:
-    def __init__(self, w, posts, full, part, g1, s1, g2, s2, rr):
-        self.w, self.posts, self.full = w, posts, full
-        self.part, self.g1, self.s1, self.g2, self.s2, self.rr = part, g1, s1, g2, s2, rr
-
-    def over_col(self, lo, src, dst):
-        w = self.w
-        self.cps = []
-        for d in range(1, NCOL):
+    def __init__(self, w, full, part, g1, s1, g2, s2, send, recv):
+        self.w, self.full, self.part = w, full, part
+        self.g1, self.s1, self.g2, self.s2 = g1, s1, g2, s2
+        self.send, self.recv = send, recv
+
+    def over_col(self, i, src, dst):
+        w = self.w
+        for d in (8, 7, 9, 6, 10, 5, 11, 4, 12, 3, 13, 2, 14, 1, 15):
             to = (w.c + d) % NCOL
-            self.cps.append(self.posts.post(src(to), dst.at[w.c], self.rr.at[lo + d], (w.r, to)))
-
-    def join(self):
-        for cp in self.cps:
-            cp.wait_recv()
+            rcopy(src(to), dst.at[w.c], self.send.at[i], self.recv.at[i], (w.r, to)).start()
+
+    def over_row(self, i, src, dst):
+        w = self.w
+        for d in (4, 3, 5, 2, 6, 1, 7):
+            to = (w.r + d) % NROW
+            rcopy(src, dst.at[w.r], self.send.at[i], self.recv.at[i], (to, w.c)).start()
+
+    def all_of(self, i, ref, count):
+        part = ref.at[pl.ds(0, count - 1)]
+        return rcopy(part, part, self.send.at[i], self.recv.at[i], (self.w.r, self.w.xc(1)))
 
     def phase1(self):
         w = self.w
@@ -305,27 +304,31 @@
 
     def phase2(self):
         w = self.w
-        self.join()
+        self.all_of(0, self.g1, NCOL).wait_recv()
         total = self.g1[0]
         for i in range(1, NCOL):
             total = total + self.g1[i]
         self.s1[...] = total
-        self.cps = []
-        for d in range(1, NROW):
-            to = ((w.r + d) % NROW, w.c)
-            self.cps.append(self.posts.post(self.s1, self.g2.at[w.r], self.rr.at[NCOL + d], to))
+        self.over_row(1, self.s1, self.g2)
         self.g2[w.r] = total
 
     def phase3(self):
         w = self.w
-        self.join()
+        self.all_of(1, self.g2, NROW).wait_recv()
         total = self.g2[0]
         for i in range(1, NROW):
             total = total + self.g2[i]
         total = total * (1.0 / (2 * GROUP * NROW * NCOL))
         self.s2[...] = total
-        self.over_col(NCOL + NROW, lambda to: self.s2, self.full)
+        self.over_col(2, lambda to: self.s2, self.full)
         self.full[w.c] = total
+
+    def join(self):
+        self.all_of(2, self.full, NCOL).wait_recv()
+
+    def drain(self):
+        for i, ref in enumerate((self.g1, self.g2, self.full)):
+            self.all_of(i, ref, NROW if i == 1 else NCOL).wait_send()
 
 
 GRAM_SCRATCH = [
@@ -334,7 +337,8 @@
     pltpu.VMEM((8, NV), F32),
     pltpu.VMEM((NROW, 8, NV), F32),
     pltpu.VMEM((8, NV), F32),
-    pltpu.SemaphoreType.DMA((2 * NCOL + NROW,)),
+    pltpu.SemaphoreType.DMA((3,)),
+    pltpu.SemaphoreType.DMA((3,)),
 ]
 NG = len(GRAM_SCRATCH)
 NR = len(RS_SCRATCH)
@@ -461,7 +465,7 @@
 
         lax.fori_loop(0, NCOL, one, 0, unroll=4)
 
-    def direct(self, rows):
+    def direct(self, lo, hi):
         def step(i, carry):
             for b in range(CHUNK):
                 k = i * CHUNK + b
@@ -469,8 +473,9 @@
                 self.chain[k + 1] = d[:, :NV] + d[:, NV:] + self.chain[self.links[0, k]]
             return carry
 
-        lax.fori_loop(0, self.steps, step, 0)
-
+        lax.fori_loop(lo, hi, step, 0)
+
+    def summed(self, rows):
         def out(i, carry):
             for h in (0, 1):
                 rows[i, pl.ds(h * BLK, BLK)] = self.chain[self.ends[0, 2 * i + h]]
@@ -512,93 +517,132 @@
 NA = len(APP_SCRATCH)
 
 
-def whole_kernel(places, links, ends, blocks, vec, out, sem, flat, chain, wcol, xrow, rows, cols, pool, work, *scratch):
+def whole_kernel(
+    places, links, ends, blocks, vec, out, sem, flat, chain, wcol, xrow, rows, cols, pool1, pool2, pool3, work, *scratch
+):
     w = Where()
     tile = Tile(places, links, ends, blocks, sem, flat, chain, wcol, xrow)
+    n = tile.steps
     tile.fetch()
-    entry_barrier(w.all_group())
-    posts = Posts(pool)
+    entry_barrier(w.neighbours())
+    posts1, posts2, posts3 = Posts(pool1), Posts(pool2), Posts(pool3)
 
     class App:
-        def __init__(self, refs, up, lo):
-            self.rowbuf, self.colbuf, ru, rl = refs[:4]
-            self.rs = refs[4 : 4 + NR]
-            self.full = refs[4 + NR]
-            self.gram = GramSum(w, posts, self.full, *refs[5 + NR :])
-            self.part = refs[5 + NR]
-            self.g = Gather(w, posts, up, lo, self.rowbuf, self.colbuf, ru, rl)
-
-        def apply(self, on_lower, on_upper, beside):
-            self.g.rest_l()
-            tile.take_cols(self.colbuf)
-            tile.direct(rows)
-
-            def flip(i):
-                if i == 0:
-                    self.g.rest_u()
-                    tile.take_rows(self.rowbuf)
-                    tile.flip(0, tile.steps // 2)
-                else:
-                    tile.flip(tile.steps // 2, tile.steps)
-                    tile.flipped(cols)
-
-            reduce_scatter(w, posts, rows, cols, self.rs, flip, on_lower, on_upper, beside)
-
-        def product(self, y):
-            self.part[...] = (self_product(y[0]) + self_product(y[1])).reshape(NCOL, 8, NV)
-
-    one = App(scratch[:NA], vec.at[0], vec.at[1])
-    two = App(scratch[NA : 2 * NA], out.at[0], out.at[1])
-    third = tile.steps // 3
-    one.g.start_l()
-    one.g.start_u()
+        def __init__(self, refs, up, lo, gather_posts, scatter_posts):
+            self.rowbuf, self.colbuf = refs[:2]
+            at = 2 + NS
+            self.full = refs[at + NR]
+            self.part = refs[at + NR + 1]
+            self.g = Gather(w, gather_posts, up, lo, self.rowbuf, self.colbuf, *refs[2:at])
+            self.s = Scatter(w, scatter_posts, rows, cols, refs[at : at + NR])
+            self.gram = GramSum(w, self.full, *refs[at + NR + 1 :])
+
+    one = App(scratch[:NA], vec.at[0], vec.at[1], posts1, posts1)
+    two = App(scratch[NA : 2 * NA], out.at[0], out.at[1], posts2, posts3)
+
+    g, s = one.g, one.s
+    g.start_y_u()
+    g.start_y_l()
+    g.start_l()
+    g.start_u()
     tile.clear()
-    tile.convert(0, third)
-    one.g.from_y_l()
-    one.g.from_y_u()
-    tile.convert(third, 2 * third)
-    one.g.from_x(False)
-    tile.convert(2 * third, tile.steps)
-    one.g.from_x(True)
-
-    def lower_one(v):
-        out[1] = v * LIFT
-        two.g.start_l()
-
-    def upper_one(v):
-        out[0] = v * LIFT
-        two.g.start_u()
-
-    one.apply(lower_one, upper_one, lambda i: None)
-    one.product(out)
+    tile.convert(0, 3)
+    g.from_y_l()
+    g.from_y_u()
+    tile.convert(3, 6)
+    g.from_x(False)
+    tile.convert(6, n)
+    g.rest_l()
+    tile.take_cols(one.colbuf)
+    tile.direct(0, 3)
+    g.from_x(True, (1,))
+    tile.direct(3, 6)
+    g.from_x(True, (3, 2))
+    tile.direct(6, n)
+    tile.summed(rows)
+    s.siblings()
+    g.rest_u()
+    tile.take_rows(one.rowbuf)
+    tile.flip(0, 3)
+    s.far_x()
+    tile.flip(3, 6)
+    s.join(4, 5)
+    s.x.through(1)
+    s.x.near(0)
+    tile.flip(6, n)
+    s.join(6, 7)
+    s.x.through(0)
+    tile.flipped(cols)
+    s.far_z()
+    s.to_y_x()
+    s.z.through(1)
+    s.z.near(0)
+    s.z.through(0)
+    s.own(1, s.x)
+    out[0] = s.final(1) * LIFT
+    g = two.g
+    g.start_y_u()
+    g.start_u()
+    s.to_y_z()
+    part = self_product(out[0])
+    s.own(0, s.z)
+    out[1] = s.final(0) * LIFT
+    g.start_y_l()
+    g.start_l()
+    one.part[...] = (part + self_product(out[1])).reshape(NCOL, 8, NV)
     one.gram.phase1()
-    two.g.from_y_u()
-    two.g.from_y_l()
+
+    s = two.s
+    g.from_y_u()
+    g.from_x(False)
+    g.from_y_l()
     one.gram.phase2()
-    two.g.from_x(False)
+    g.from_x(True)
+    g.rest_u()
+    tile.take_rows(two.rowbuf)
+    tile.flip(0, n // 2)
     one.gram.phase3()
-    two.g.from_x(True)
+    tile.flip(n // 2, n)
+    posts1.drain()
+    tile.flipped(cols)
+    s.far_z()
+    g.rest_l()
+    tile.take_cols(two.colbuf)
+    tile.direct(0, n // 2)
+    s.z.through(1)
+    s.z.near(0)
+    tile.direct(n // 2, n)
+    s.z.through(0)
+    tile.summed(rows)
+    s.siblings()
     one.gram.join()
-    posts.drain()
-
-    def beside(i):
-        state = one.full[...].reshape(NV, NV) if i == 0 else work[...]
-        work[...] = eliminate(state, 4 * i, 4 * i + 4)
-
-    def lower_two(v):
-        out[1] = times_inverse(v, lower_part(work[...]))
-
-    def upper_two(v):
-        out[0] = times_inverse(v, lower_part(work[...]))
-
-    two.apply(lower_two, upper_two, beside)
-    two.product(out)
+    one.gram.drain()
+    work[...] = eliminate(one.full[...].reshape(NV, NV), 0, 4)
+    s.far_x()
+    s.join(4, 5)
+    work[...] = eliminate(work[...], 4, 8)
+    s.x.through(1)
+    s.x.near(0)
+    s.join(6, 7)
+    s.x.through(0)
+    s.to_y_z()
+    work[...] = eliminate(work[...], 8, 12)
+    s.own(0, s.z)
+    s.to_y_x()
+    work[...] = lower_part(eliminate(work[...], 12, 16))
+    posts2.drain()
+    out[1] = times_inverse(s.final(0), work[...])
+    part = self_product(out[1])
+    s.own(1, s.x)
+    out[0] = times_inverse(s.final(1), work[...])
+    two.part[...] = (part + self_product(out[0])).reshape(NCOL, 8, NV)
     two.gram.phase1()
     two.gram.phase2()
     two.gram.phase3()
     two.gram.join()
     linv = lower_part(eliminate(two.full[...].reshape(NV, NV), 0, 16))
-    posts.drain()
+    two.gram.drain()
+    posts3.drain()
     out[0] = times_inverse(out[0], linv)
     out[1] = times_inverse(out[1], linv)
 
@@ -632,9 +676,9 @@
             pltpu.VMEM((32, NV, 2 * BLK), BF16),
             pltpu.VMEM((NCOL, GROUP, NV), F32),
             pltpu.VMEM((NROW, GROUP, NV), F32),
-            POOL,
-            pltpu.VMEM((NV, NV), F32),
         ]
+        + POOLS
+        + [pltpu.VMEM((NV, NV), F32)]
         + APP_SCRATCH
         + APP_SCRATCH,
         compiler_params=pltpu.CompilerParams(

time: 125 us -> 116 us (0.928)
  Pallas kernels: 123 us -> 114 us
    pallas_call x1, Pallas kernels: 121 us -> 112 us  [local(): pl.pallas_call(whole_kernel, out_shape=jax.ShapeDtypeStruct((2, GROUP, NV...]
where the time goes in v4:
time: 116 us
  Pallas kernels  114 us (98%)
  local copies, waits for them, and re-layouts  1.67 us (1%)
    pallas_call x1, Pallas kernels, local(): pl.pallas_call(whole_kernel, out_shape=jax.ShapeDtypeStruct((2, GROUP, NV...  112 us

profile of v4, /device:TPU:1, one launch (start us, length us, event | category | flops | bytes accessed | tf_op | source)
XLA Modules:
  0.0 115.9 jit_solution(4565403904428590588)
XLA Ops:
  0.0 1.9 %links.1 = (s32[2,170]{1,0:T(2,128)}, s32[2,32]{1,0:T(2,128)}) custom-call(s32[2,170]{1,0:T(2,128)} %bitcast.3), custom_call_target="tpu_custom_call" | custom-call | tf_op jit(solution)/shard_map/links/pallas_call | solution.py:655
  1.9 112.4 %whole.1 = f32[2,256,128]{2,1,0:T(8,128)} custom-call(s32[2,170]{1,0:T(2,128)} %bitcast.4, s32[2,170]{1,0:T(2,128)} %get-tuple-element.7.links, s32[2,32]{1,0:T(2,128)} %get-tuple-element.8.ends, f32[170,128,128]{2,1,0:T(8,128)} %bitcast.2, f32[2,256,128]{2,1,0:T(8,128)} %vec.1), custom_call_target="tpu_custom_call" | custom-call | tf_op jit(solution)/shard_map/whole/pallas_call | solution.py:666
  114.3 1.7 %copy.5 = f32[2,256,128]{2,1,0:T(8,128)} copy(f32[2,256,128]{2,1,0:T(8,128)} %whole.1) | data formatting | bytes 524288

commit v5 on v4

--- a/solution.py
+++ b/solution.py
@@ -395,23 +395,21 @@
     return hi, lo
 
 
-def link_kernel(places, links, ends, last_row, last_col):
-    listed = places.shape[1]
-    for i in range(32):
-        last_row[i] = 0
-    for i in range(16):
-        last_col[i] = 0
-    for k in range(listed):
-        r = places[0, k]
-        c = places[1, k]
-        links[0, k] = last_row[r]
-        links[1, k] = last_col[c]
-        last_row[r] = k + 1
-        last_col[c] = k + 1
-    for i in range(32):
-        ends[0, i] = last_row[i]
-    for i in range(16):
-        ends[1, i] = last_col[i]
+def link_tables(coords, links, ends):
+    listed = coords.shape[1]
+    lane = lax.broadcasted_iota(jnp.int32, (listed, listed), 1)
+    sub = lax.broadcasted_iota(jnp.int32, (listed, listed), 0)
+    count = lax.broadcasted_iota(jnp.int32, (listed, NV), 0) + 1
+    place = lax.broadcasted_iota(jnp.int32, (listed, NV), 1)
+    links[...] = jnp.zeros(links.shape, jnp.int32)
+    ends[...] = jnp.zeros(ends.shape, jnp.int32)
+    for t in (0, 1):
+        along = jnp.broadcast_to(coords[t : t + 1, :], (listed, listed))
+        down = jnp.max(jnp.where(lane == sub, along, 0), axis=1, keepdims=True)
+        before = jnp.logical_and(jnp.broadcast_to(down, (listed, listed)) == along, sub < lane)
+        links[t : t + 1, :listed] = jnp.max(jnp.where(before, sub + 1, 0), axis=0, keepdims=True)
+        here = jnp.broadcast_to(down, (listed, NV)) == place
+        ends[t : t + 1, :] = jnp.max(jnp.where(here, count, 0), axis=0, keepdims=True)
 
 
 class Tile:
@@ -518,7 +516,7 @@
 
 
 def whole_kernel(
-    places, links, ends, blocks, vec, out, sem, flat, chain, wcol, xrow, rows, cols, pool1, pool2, pool3, work, *scratch
+    places, coords, blocks, vec, out, links, ends, vlinks, vends, s_tab, sem, flat, chain, wcol, xrow, rows, cols, pool1, pool2, pool3, work, *scratch
 ):
     w = Where()
     tile = Tile(places, links, ends, blocks, sem, flat, chain, wcol, xrow)
@@ -541,10 +539,17 @@
     two = App(scratch[NA : 2 * NA], out.at[0], out.at[1], posts2, posts3)
 
     g, s = one.g, one.s
+    g.start_y_l()
     g.start_y_u()
-    g.start_y_l()
     g.start_l()
     g.start_u()
+    link_tables(coords, vlinks, vends)
+    tables = [
+        pltpu.make_async_copy(vlinks, links, s_tab.at[0]),
+        pltpu.make_async_copy(vends, ends, s_tab.at[1]),
+    ]
+    for t in tables:
+        t.start()
     tile.clear()
     tile.convert(0, 3)
     g.from_y_l()
@@ -552,6 +557,8 @@
     tile.convert(3, 6)
     g.from_x(False)
     tile.convert(6, n)
+    for t in tables:
+        t.wait()
     g.rest_l()
     tile.take_cols(one.colbuf)
     tile.direct(0, 3)
@@ -615,15 +622,15 @@
     s.z.through(0)
     tile.summed(rows)
     s.siblings()
+    s.far_x()
+    s.join(4, 5)
     one.gram.join()
     one.gram.drain()
     work[...] = eliminate(one.full[...].reshape(NV, NV), 0, 4)
-    s.far_x()
-    s.join(4, 5)
-    work[...] = eliminate(work[...], 4, 8)
     s.x.through(1)
     s.x.near(0)
     s.join(6, 7)
+    work[...] = eliminate(work[...], 4, 8)
     s.x.through(0)
     s.to_y_z()
     work[...] = eliminate(work[...], 8, 12)
@@ -652,23 +659,17 @@
     places = coords.reshape(2, coords.shape[3])
     listed = values.shape[0]
     scalars = pl.BlockSpec(memory_space=pltpu.SMEM)
-    links, ends = pl.pallas_call(
-        link_kernel,
-        out_shape=(
-            jax.ShapeDtypeStruct((2, listed), jnp.int32),
-            jax.ShapeDtypeStruct((2, 32), jnp.int32),
-        ),
-        in_specs=[scalars],
-        out_specs=(scalars, scalars),
-        scratch_shapes=[pltpu.SMEM((32,), jnp.int32), pltpu.SMEM((16,), jnp.int32)],
-        name="links",
-    )(places)
     return pl.pallas_call(
         whole_kernel,
         out_shape=jax.ShapeDtypeStruct((2, GROUP, NV), F32),
-        in_specs=[scalars] * 3 + [pl.BlockSpec(memory_space=pl.ANY), VM],
+        in_specs=[scalars, VM, pl.BlockSpec(memory_space=pl.ANY), VM],
         out_specs=VM,
         scratch_shapes=[
+            pltpu.SMEM((8, 256), jnp.int32),
+            pltpu.SMEM((8, NV), jnp.int32),
+            pltpu.VMEM((8, 256), jnp.int32),
+            pltpu.VMEM((8, NV), jnp.int32),
+            pltpu.SemaphoreType.DMA((2,)),
             pltpu.SemaphoreType.DMA((listed // CHUNK,)),
             pltpu.VMEM((listed, BLK, 2 * BLK), BF16),
             pltpu.VMEM((listed + 1, BLK, BLK), F32),
@@ -685,7 +686,7 @@
             collective_id=0, has_side_effects=True, vmem_limit_bytes=56 << 20
         ),
         name="whole",
-    )(places, links, ends, values, vectors)
+    )(places, places, values, vectors)
 
 
 def solution(mesh):

time: 116 us -> 112 us (0.966)
  Pallas kernels: 114 us -> 110 us
    pallas_call x1, Pallas kernels: 112 us -> 110 us  [local(): pl.pallas_call(whole_kernel, out_shape=jax.ShapeDtypeStruct((2, GROUP, NV...]
    pallas_call x1 -> x0, Pallas kernels: 1.85 us -> none  [local(): pl.pallas_call(link_kernel, out_shape=(jax.ShapeDtypeStruct((2, listed),...]
where the time goes in v5:
time: 112 us
  Pallas kernels  110 us (98%)
  local copies, waits for them, and re-layouts  1.67 us (1%)
    pallas_call x1, Pallas kernels, local(): pl.pallas_call(whole_kernel, out_shape=jax.ShapeDtypeStruct((2, GROUP, NV...  110 us

profile of v5, /device:TPU:1, one launch (start us, length us, event | category | flops | bytes accessed | tf_op | source)
XLA Modules:
  0.0 112.0 jit_solution(1886434634337938876)
XLA Ops:
  0.0 110.3 %whole.1 = f32[2,256,128]{2,1,0:T(8,128)} custom-call(s32[2,170]{1,0:T(2,128)} %bitcast.3, s32[2,170]{1,0:T(2,128)} %bitcast.4, f32[170,128,128]{2,1,0:T(8,128)} %bitcast.2, f32[2,256,128]{2,1,0:T(8,128)} %vec.1), custom_call_target="tpu_custom_call" | custom-call | tf_op jit(solution)/shard_map/whole/pallas_call | solution.py:662
  110.3 1.7 %copy.5 = f32[2,256,128]{2,1,0:T(8,128)} copy(f32[2,256,128]{2,1,0:T(8,128)} %whole.1) | data formatting | bytes 524288

commit v6 on v5

--- a/solution.py
+++ b/solution.py
@@ -572,15 +572,14 @@
     tile.take_rows(one.rowbuf)
     tile.flip(0, 3)
     s.far_x()
-    tile.flip(3, 6)
     s.join(4, 5)
+    tile.flip(3, n)
+    tile.flipped(cols)
+    s.far_z()
     s.x.through(1)
     s.x.near(0)
-    tile.flip(6, n)
     s.join(6, 7)
     s.x.through(0)
-    tile.flipped(cols)
-    s.far_z()
     s.to_y_x()
     s.z.through(1)
     s.z.near(0)
@@ -603,26 +602,24 @@
     g.from_y_u()
     g.from_x(False)
     g.from_y_l()
+    g.from_x(True)
     one.gram.phase2()
-    g.from_x(True)
     g.rest_u()
     tile.take_rows(two.rowbuf)
-    tile.flip(0, n // 2)
-    one.gram.phase3()
-    tile.flip(n // 2, n)
+    tile.flip(0, n)
     posts1.drain()
     tile.flipped(cols)
     s.far_z()
+    one.gram.phase3()
     g.rest_l()
     tile.take_cols(two.colbuf)
-    tile.direct(0, n // 2)
+    tile.direct(0, n)
+    tile.summed(rows)
+    s.siblings()
     s.z.through(1)
     s.z.near(0)
-    tile.direct(n // 2, n)
+    s.far_x()
     s.z.through(0)
-    tile.summed(rows)
-    s.siblings()
-    s.far_x()
     s.join(4, 5)
     one.gram.join()
     one.gram.drain()

time: 112 us -> 109 us (0.973)
  Pallas kernels: 110 us -> 107 us
    pallas_call x1, Pallas kernels: 110 us -> 107 us  [local(): pl.pallas_call(whole_kernel, out_shape=jax.ShapeDtypeStruct((2, GROUP, NV...]
where the time goes in v6:
time: 109 us
  Pallas kernels  107 us (98%)
  local copies, waits for them, and re-layouts  1.67 us (2%)
    pallas_call x1, Pallas kernels, local(): pl.pallas_call(whole_kernel, out_shape=jax.ShapeDtypeStruct((2, GROUP, NV...  107 us

profile of v6, /device:TPU:1, one launch (start us, length us, event | category | flops | bytes accessed | tf_op | source)
XLA Modules:
  0.0 108.5 jit_solution(10372633337968744228)
XLA Ops:
  0.0 106.8 %whole.1 = f32[2,256,128]{2,1,0:T(8,128)} custom-call(s32[2,170]{1,0:T(2,128)} %bitcast.3, s32[2,170]{1,0:T(2,128)} %bitcast.4, f32[170,128,128]{2,1,0:T(8,128)} %bitcast.2, f32[2,256,128]{2,1,0:T(8,128)} %vec.1), custom_call_target="tpu_custom_call" | custom-call | tf_op jit(solution)/shard_map/whole/pallas_call | solution.py:659
  106.8 1.7 %copy.5 = f32[2,256,128]{2,1,0:T(8,128)} copy(f32[2,256,128]{2,1,0:T(8,128)} %whole.1) | data formatting | bytes 524288

commit v7 on v6

--- a/solution.py
+++ b/solution.py
@@ -580,9 +580,9 @@
     s.x.near(0)
     s.join(6, 7)
     s.x.through(0)
-    s.to_y_x()
     s.z.through(1)
     s.z.near(0)
+    s.to_y_x()
     s.z.through(0)
     s.own(1, s.x)
     out[0] = s.final(1) * LIFT

time: 109 us -> 108 us (level)
  no operation moved by 1% of the time
where the time goes in v7:
time: 108 us
  Pallas kernels  107 us (99%)
  local copies, waits for them, and re-layouts  1.67 us (2%)
    pallas_call x1, Pallas kernels, local(): pl.pallas_call(whole_kernel, out_shape=jax.ShapeDtypeStruct((2, GROUP, NV...  107 us

profile of v7, /device:TPU:1, one launch (start us, length us, event | category | flops | bytes accessed | tf_op | source)
XLA Modules:
  0.0 108.3 jit_solution(2214247144427254328)
XLA Ops:
  0.0 106.6 %whole.1 = f32[2,256,128]{2,1,0:T(8,128)} custom-call(s32[2,170]{1,0:T(2,128)} %bitcast.3, s32[2,170]{1,0:T(2,128)} %bitcast.4, f32[170,128,128]{2,1,0:T(8,128)} %bitcast.2, f32[2,256,128]{2,1,0:T(8,128)} %vec.1), custom_call_target="tpu_custom_call" | custom-call | tf_op jit(solution)/shard_map/whole/pallas_call | solution.py:659
  106.6 1.7 %copy.5 = f32[2,256,128]{2,1,0:T(8,128)} copy(f32[2,256,128]{2,1,0:T(8,128)} %whole.1) | data formatting | bytes 524288
